TPU v7x, 512 devices: a whole 4x8x8 slice. The times are simulated.
512 devices in a mesh: dp: 256 (over z, y, x), ctx: 2 (over core).
Axes of the slice: x: 4, y: 8, z: 8, core: 2. Of those that a mesh axis runs over, the one named last changes fastest.
Arguments:
- head_inputs: bfloat16 [256, 512, 1024], P('dp', 'ctx'), may hold values from -6 to 6
- cotangent: bfloat16 [256, 512, 1024], P('dp', 'ctx'), may hold values from -6 to 6
- write_proj: bfloat16 [256, 512, 256], P('dp', 'ctx'), may hold values from -3 to 3
- read_proj: bfloat16 [256, 512, 256], P('dp', 'ctx'), may hold values from -3 to 3
- step_raw: float32 [256, 512, 16], P('dp', 'ctx'), may hold values from -4 to 4
- doc_index: int32 [256, 512], P('dp', 'ctx'), may hold values from 0 to 15, never falling along the last dimension, each value on 1 to 257 neighbouring positions
- log_rate: float32 [16], replicated, may hold values from 0 to 2.77
- step_bias: float32 [16], replicated, may hold values from -6.9 to -2.25
- skip_gain: float32 [16], replicated, may hold values from 0.5 to 1.5
Outputs:
- grad_inputs: bfloat16 [256, 512, 1024], P('dp', 'ctx')
- grad_write: bfloat16 [256, 512, 256], P('dp', 'ctx')
- grad_read: bfloat16 [256, 512, 256], P('dp', 'ctx')
- grad_step: float32 [256, 512, 16], P('dp', 'ctx')
- grad_rate: float32 [16], replicated
- grad_bias: float32 [16], replicated
- grad_skip: float32 [16], replicated
Inputs may be any that keep to these rules, and one draw needn't show every extreme that they name: doc_index never falls along a sequence; each document spans 1 to 257 tokens and one of each sequence spans exactly that many.
All inputs are finite; a program needn't handle non-finite values.
Results may differ from a plain program's by a relative error of at most 0.0025.
Values may be sent and summed in bfloat16 or wider, within the bound.
No kernel may reach another device: no remote copies, remote signals or barrier semaphores. Data moves between devices by JAX's collectives and lax.ppermute only.
A program may use at most 64 MiB of HBM per device.

v0:
```python
import jax
import jax.numpy as jnp
from jax import lax
from jax.sharding import PartitionSpec as P

HEADS = 16
HEAD_DIM = 64
STATE = 256
BLOCK = 256


def ssd_forward(
    inputs, writes, reads, steps, segment, segment_prev, state_init, log_rate, skip_gain
):
    length, heads, width = inputs.shape
    count = length // BLOCK
    rate_all = steps * (-jnp.exp(log_rate))[None, :]
    blocks = (
        inputs.reshape(count, BLOCK, heads, width),
        writes.reshape(count, BLOCK, -1),
        reads.reshape(count, BLOCK, -1),
        steps.reshape(count, BLOCK, heads),
        rate_all.reshape(count, BLOCK, heads),
        segment.reshape(count, BLOCK),
    )
    causal = jnp.arange(BLOCK)[:, None] >= jnp.arange(BLOCK)[None, :]
    highest = lax.Precision.HIGHEST

    def advance(carry, piece):
        state, last_doc = carry
        in_block, write_block, read_block, step_block, rate_block, doc_block = piece
        cumulative = jnp.cumsum(rate_block, axis=0)
        same_doc = causal & (doc_block[:, None] == doc_block[None, :])
        gaps = cumulative[:, None, :] - cumulative[None, :, :]
        decay = jnp.exp(jnp.where(same_doc[:, :, None], gaps, -1e30))
        scores = jnp.einsum("in,jn->ij", read_block, write_block, precision=highest)
        mixing = decay * (scores[:, :, None] * step_block[None, :, :])
        result = jnp.einsum("ijh,jhp->ihp", mixing, in_block, precision=highest)
        keep = (doc_block == last_doc).astype(jnp.float32)
        start = jnp.exp(cumulative) * keep[:, None]
        result = (
            result
            + jnp.einsum("in,hpn->ihp", read_block, state, precision=highest) * start[:, :, None]
        )
        result = result + skip_gain[None, :, None] * in_block
        end_doc = doc_block[BLOCK - 1]
        tail = (
            jnp.exp(cumulative[BLOCK - 1][None, :] - cumulative)
            * (doc_block == end_doc).astype(jnp.float32)[:, None]
            * step_block
        )
        carried = jnp.exp(cumulative[BLOCK - 1]) * (end_doc == last_doc).astype(jnp.float32)
        state = carried[:, None, None] * state + jnp.einsum(
            "jh,jhp,jn->hpn", tail, in_block, write_block, precision=highest
        )
        return ((state, end_doc), result)

    (state, _), results = lax.scan(jax.checkpoint(advance), (state_init, segment_prev), blocks)
    return (results.reshape(length, heads, width), state)


def layer_grads(
    inputs,
    cotangent,
    writes,
    reads,
    step_raw,
    segment,
    segment_prev,
    state_init,
    log_rate,
    step_bias,
    skip_gain,
    state_grad,
):
    length = inputs.shape[0]
    heads = step_raw.shape[1]
    head_view = inputs.astype(jnp.float32).reshape(length, heads, HEAD_DIM)

    def forward(head_view, writes, reads, step_raw, log_rate, step_bias, skip_gain):
        steps = jax.nn.softplus(step_raw + step_bias[None, :])
        return ssd_forward(
            head_view, writes, reads, steps, segment, segment_prev, state_init, log_rate, skip_gain
        )

    _, pullback = jax.vjp(
        forward,
        head_view,
        writes.astype(jnp.float32),
        reads.astype(jnp.float32),
        step_raw,
        log_rate,
        step_bias,
        skip_gain,
    )
    return pullback((cotangent.astype(jnp.float32).reshape(length, heads, HEAD_DIM), state_grad))


def on_device(
    head_inputs,
    cotangent,
    write_proj,
    read_proj,
    step_raw,
    doc_index,
    log_rate,
    step_bias,
    skip_gain,
):
    group_size = lax.axis_size("ctx")
    per_device = HEADS // group_size
    first_head = lax.axis_index("ctx") * per_device
    head_rows, cotan_rows = (
        lax.all_to_all(head_inputs, "ctx", split_axis=2, concat_axis=1, tiled=True),
        lax.all_to_all(cotangent, "ctx", split_axis=2, concat_axis=1, tiled=True),
    )
    raw_steps = lax.all_to_all(step_raw, "ctx", split_axis=2, concat_axis=1, tiled=True)
    write_all, read_all = (
        lax.all_gather(write_proj, "ctx", axis=1, tiled=True),
        lax.all_gather(read_proj, "ctx", axis=1, tiled=True),
    )
    segment = lax.all_gather(doc_index, "ctx", axis=1, tiled=True)[0]
    length = segment.shape[0]
    rate_here = lax.dynamic_slice_in_dim(log_rate, first_head, per_device)
    bias_here = lax.dynamic_slice_in_dim(step_bias, first_head, per_device)
    skip_here = lax.dynamic_slice_in_dim(skip_gain, first_head, per_device)
    zero_state = jnp.zeros((per_device, HEAD_DIM, STATE), jnp.float32)
    grads = layer_grads(
        head_rows[0],
        cotan_rows[0],
        write_all[0],
        read_all[0],
        raw_steps[0],
        segment,
        segment[0],
        zero_state,
        rate_here,
        bias_here,
        skip_here,
        zero_state,
    )
    out_inputs = lax.all_to_all(
        grads[0].reshape(1, length, per_device * HEAD_DIM).astype(jnp.bfloat16),
        "ctx",
        split_axis=1,
        concat_axis=2,
        tiled=True,
    )
    out_step = lax.all_to_all(grads[3][None], "ctx", split_axis=1, concat_axis=2, tiled=True)
    sum_write, sum_read = (
        lax.psum_scatter(grads[1][None], "ctx", scatter_dimension=1, tiled=True),
        lax.psum_scatter(grads[2][None], "ctx", scatter_dimension=1, tiled=True),
    )
    out_write = sum_write.astype(jnp.bfloat16)
    out_read = sum_read.astype(jnp.bfloat16)

    def place(values):
        return lax.dynamic_update_slice_in_dim(
            jnp.zeros((HEADS,), jnp.float32), values, first_head, 0
        )

    partial_sums = (place(grads[4]), place(grads[5]), place(grads[6]))
    total_rate, total_bias, total_skip = lax.psum(
        (partial_sums[0], partial_sums[1], partial_sums[2]), ("dp", "ctx")
    )
    return (out_inputs, out_write, out_read, out_step, total_rate, total_bias, total_skip)


def solution(mesh):
    placed = (
        P("dp", "ctx", None),
        P("dp", "ctx", None),
        P("dp", "ctx", None),
        P("dp", "ctx", None),
        P("dp", "ctx", None),
        P("dp", "ctx"),
        P(),
        P(),
        P(),
    )
    return jax.shard_map(
        on_device,
        mesh=mesh,
        in_specs=placed,
        out_specs=(
            P("dp", "ctx", None),
            P("dp", "ctx", None),
            P("dp", "ctx", None),
            P("dp", "ctx", None),
            P(),
            P(),
            P(),
        ),
        check_vma=False,
    )
```

profile of v0, /device:TPU:1, one launch (start us, length us, event | category | flops | bytes accessed | tf_op | source)
XLA Modules:
  0.0 267.5 jit_solution(3828304413454677464)
XLA Ops:
  7.2 2.4 copy.57
  10.2 3.9 %reduce.18 = bf16[1024,256]{1,0:T(8,128)(2,1)S(1)} reduce(bf16[1024,1,256]{2,1,0:T(2,128)(2,1)S(1)} %bitcast.276, bf16[]{:T(256)} %broadcast.266), dimensions={1}, to_apply=%bitcast.160.reduce_sub_computation | reduce | bytes 1048578
  15.0 10.5 %all-to-all-start.1 = ((bf16[2,2,65536]{2,1,0:T(2,128)(2,1)}), bf16[2,2,65536]{2,1,0:T(2,128)(2,1)S(1)}, u32[]{:S(2)}, u32[]{:S(2)}) async-start(bf16[2,2,65536]{2,1,0:T(2,128)(2,1)} %reshape.420), calls=%async_computation.1 | async-start | bytes 1048576 | tf_op jit(solution)/shard_map/all_to_all | solution.py:114
  26.2 1.8 all_gather.9
  30.4 2.0 all_gather.10
  32.4 2.0 all_gather.11
  34.4 2.4 copy.58
  36.8 4.7 %reduce.19 = bf16[1024,256]{1,0:T(8,128)(2,1)} reduce(bf16[1024,1,256]{2,1,0:T(2,128)(2,1)S(1)} %bitcast.280, bf16[]{:T(256)} %broadcast.266), dimensions={1}, to_apply=%bitcast.162.reduce_sub_computation | reduce | bytes 1048578
  41.5 1.8 reshape.422
  43.3 4.4 %all-to-all-start.2 = ((bf16[2,2,65536]{2,1,0:T(2,128)(2,1)}), bf16[2,2,65536]{2,1,0:T(2,128)(2,1)}, u32[]{:S(2)}, u32[]{:S(2)}) async-start(bf16[2,2,65536]{2,1,0:T(2,128)(2,1)} %reshape.422), calls=%async_computation.2 | async-start | bytes 1048576 | tf_op jit(solution)/shard_map/all_to_all | solution.py:115
  50.4 3.3 %all-to-all-start = ((f32[1,256,16]{1,0,2:T(1,128)}), f32[1,256,16]{1,0,2:T(1,128)S(1)}, u32[]{:S(2)}, u32[]{:S(2)}) async-start(f32[1,256,16]{1,0,2:T(1,128)} %copy.56), calls=%async_computation | async-start | bytes 32768 | tf_op jit(solution)/shard_map/all_to_all | solution.py:117
  53.8 1.4 reshape.423
  58.1 13.2 %while.44 = (s32[]{:T(128)}, f32[8,64,256]{2,1,0:T(8,128)S(1)}, s32[]{:T(128)}, f32[2,8,64,256]{3,2,1,0:T(8,128)}, s32[2]{0:T(128)S(1)}, /*index=5*/f32[2,256,8]...) while((s32[]{:T(128)}, f32[8,64,256]{2,1,0:T(8,128)S(1)}, ...), condition=%wide.region_3.4_spmd.clone, body=%wide.region_0.3_spmd.clone.sunk | while | flops 403577376 | bytes 2971505 | solution.py:58
  62.8 1.9 convolution_add_fusion.6
  69.4 1.9 convolution_add_fusion.6
  75.0 60.5 %while.45 = (s32[]{:T(128)}, f32[8]{0:T(128)}, f32[8,64,256]{2,1,0:T(8,128)}, bf16[2,256,8,64]{1,3,2,0:T(8,128)(2,1)}, f32[2,256,256]{2,1,0:T(8,128)}, /*index=5...) while((s32[]{:T(128)}, f32[8]{0:T(128)}, ...), condition=%wide.region_17.18_spmd.clone, body=%wide.region_4.0_spmd.clone.sunk | while | flops 3434652672 | bytes 35708892 | solution.py:58
  86.1 4.1 %fusion.109 = (f32[256,8]{0,1:T(8,128)}, f32[256,8]{0,1:T(8,128)}, f32[256,8]{0,1:T(8,128)}, f32[256,256]{1,0:T(8,128)S(1)}) fusion(f32[256,8]{0,1:T(8,128)S(1)} %get-tuple-element.914, f32[256,256]{1,0:T(8,128)S(1)} %fusion.108, f32[256,8]{0,1:T(8,128)S(1)} %get-tuple-element.912, pred[256,256]{1,0:T(8,128)(4,1)S(1)} %compare_and_fusion.2, ...), kind=kOutput, calls=%fused_computation.30.clone.1 | convolution fusion | flops 409397248 | bytes 1679360 | tf_op jit(solution)/shard_map/transpose(jvp())/while/body/eval_jaxpr/checkpoint/ijh,jhp->ihp/dot_general | solution.py:38
  93.4 1.4 bitcast_dynamic-update-slice_fusion.7
  94.8 3.6 %fusion.112 = bf16[2,256,8,64]{1,3,2,0:T(8,128)(2,1)} fusion(bf16[2,256,8,64]{1,3,2,0:T(8,128)(2,1)} %get-tuple-element.993, s32[]{:T(128)S(6)} %sub.194, f32[256,8]{0,1:T(8,128)S(1)} %get-tuple-element.914, f32[256,256]{1,0:T(8,128)} %copy-done.1, f32[256,8]{0,1:T(8,128)S(1)} %get-tuple-element.912, pred[256,256]{1,0:T(8,128)(4,1)S(1)} %compare_and_fusion.2, ...), kind=kOutput, calls=%fused_computation.33.clone.1 | convolution fusion | flops 405274624 | bytes 2458116 | tf_op jit(solution)/shard_map/transpose(jvp())/while/body/eval_jaxpr/checkpoint/ijh,jhp->ihp/dot_general | solution.py:38
  99.4 1.4 convolution_add_fusion.7
  101.4 2.5 reduce-window.70
  116.9 4.0 %fusion.109 = (f32[256,8]{0,1:T(8,128)}, f32[256,8]{0,1:T(8,128)}, f32[256,8]{0,1:T(8,128)}, f32[256,256]{1,0:T(8,128)S(1)}) fusion(f32[256,8]{0,1:T(8,128)S(1)} %get-tuple-element.914, f32[256,256]{1,0:T(8,128)S(1)} %fusion.108, f32[256,8]{0,1:T(8,128)S(1)} %get-tuple-element.912, pred[256,256]{1,0:T(8,128)(4,1)S(1)} %compare_and_fusion.2, ...), kind=kOutput, calls=%fused_computation.30.clone.1 | convolution fusion | flops 409397248 | bytes 1679360 | tf_op jit(solution)/shard_map/transpose(jvp())/while/body/eval_jaxpr/checkpoint/ijh,jhp->ihp/dot_general | solution.py:38
  124.1 1.4 bitcast_dynamic-update-slice_fusion.7
  125.5 3.6 %fusion.112 = bf16[2,256,8,64]{1,3,2,0:T(8,128)(2,1)} fusion(bf16[2,256,8,64]{1,3,2,0:T(8,128)(2,1)} %get-tuple-element.993, s32[]{:T(128)S(6)} %sub.194, f32[256,8]{0,1:T(8,128)S(1)} %get-tuple-element.914, f32[256,256]{1,0:T(8,128)} %copy-done.1, f32[256,8]{0,1:T(8,128)S(1)} %get-tuple-element.912, pred[256,256]{1,0:T(8,128)(4,1)S(1)} %compare_and_fusion.2, ...), kind=kOutput, calls=%fused_computation.33.clone.1 | convolution fusion | flops 405274624 | bytes 2458116 | tf_op jit(solution)/shard_map/transpose(jvp())/while/body/eval_jaxpr/checkpoint/ijh,jhp->ihp/dot_general | solution.py:38
  130.2 1.4 convolution_add_fusion.7
  132.2 2.5 reduce-window.70
  140.1 3.3 %all-to-all-start.4 = ((f32[2,1,2048]{2,1,0:T(1,128)}), f32[2,1,2048]{2,1,0:T(1,128)S(1)}, u32[]{:S(2)}, u32[]{:S(2)}) async-start(f32[2,1,2048]{2,1,0:T(1,128)} %reshape.426), calls=%async_computation.6 | async-start | bytes 32768 | tf_op jit(solution)/shard_map/all_to_all | solution.py:149
  143.4 99.9 %all-reduce.2 = (f32[16]{0:T(128)}, f32[16]{0:T(128)}, f32[16]{0:T(128)}) all-reduce(f32[16]{0:T(128)S(1)} %multiply_dynamic-update-slice_fusion, f32[16]{0:T(128)S(1)} %dynamic_update_slice.66, f32[16]{0:T(128)S(1)} %dynamic_update_slice.67), channel_id=1, replica_groups=mesh['dp'=256,'ctx'=2] {'dp','ctx'}, use_global_device_ids=true, to_apply=%region_21.22 | all-reduce | flops 48 | bytes 384 | tf_op jit(solution)/shard_map/psum | solution.py:163
  244.6 3.9 %reduce.20 = bf16[512,512]{1,0:T(8,128)(2,1)S(1)} reduce(bf16[512,1,512]{2,1,0:T(2,128)(2,1)S(1)} %bitcast.277, bf16[]{:T(256)} %broadcast.266), dimensions={1}, to_apply=%bitcast.164.reduce_sub_computation | reduce | bytes 1048578
  249.5 4.2 %all-to-all-start.3 = ((bf16[2,2,65536]{2,1,0:T(2,128)(2,1)}), bf16[2,2,65536]{2,1,0:T(2,128)(2,1)S(1)}, u32[]{:S(2)}, u32[]{:S(2)}) async-start(bf16[2,2,65536]{2,1,0:T(2,128)(2,1)} %reshape.424), calls=%async_computation.3 | async-start | bytes 1048576 | tf_op jit(solution)/shard_map/all_to_all | solution.py:142
  257.4 1.6 convert_element_type.114
  259.0 1.6 convert_element_type.115
  (268 shorter events, 62.8 us)
Async XLA Ops:
  14.0 11.4 %copy-start.32 = (f32[16]{0:T(128)S(1)}, f32[16]{0:T(128)}, u32[]{:S(2)}) copy-start(f32[16]{0:T(128)} %param.20) | copy-start | bytes 196
  14.1 11.5 %copy-start.30 = (f32[16]{0:T(128)S(1)}, f32[16]{0:T(128)}, u32[]{:S(2)}) copy-start(f32[16]{0:T(128)} %param.19) | copy-start | bytes 196
  14.1 11.6 %copy-start.33 = (f32[16]{0:T(128)S(1)}, f32[16]{0:T(128)}, u32[]{:S(2)}) copy-start(f32[16]{0:T(128)} %param.21) | copy-start | bytes 196
  14.1 12.2 %copy-start.29 = (s32[1,256]{1,0:T(1,128)S(1)}, s32[1,256]{1,0:T(1,128)}, u32[]{:S(2)}) copy-start(s32[1,256]{1,0:T(1,128)} %param.18) | copy-start | bytes 3076
  14.1 15.6 %copy-start.20 = (f32[1,256,16]{1,2,0:T(8,128)S(1)}, f32[1,256,16]{1,2,0:T(8,128)}, u32[]{:S(2)}) copy-start(f32[1,256,16]{1,2,0:T(8,128)} %param.17) | copy-start | bytes 49156
  14.1 16.3 %copy-start.16 = (bf16[1,256,256]{2,1,0:T(8,128)(2,1)S(1)}, bf16[1,256,256]{2,1,0:T(8,128)(2,1)}, u32[]{:S(2)}) copy-start(bf16[1,256,256]{2,1,0:T(8,128)(2,1)} %param.15) | copy-start | bytes 393220
  15.0 17.4 %copy-start.17 = (bf16[1,256,256]{2,1,0:T(8,128)(2,1)S(1)}, bf16[1,256,256]{2,1,0:T(8,128)(2,1)}, u32[]{:S(2)}) copy-start(bf16[1,256,256]{2,1,0:T(8,128)(2,1)} %param.16) | copy-start | bytes 393220
  15.0 28.3 %all-to-all-start.1 = ((bf16[2,2,65536]{2,1,0:T(2,128)(2,1)}), bf16[2,2,65536]{2,1,0:T(2,128)(2,1)S(1)}, u32[]{:S(2)}, u32[]{:S(2)}) async-start(bf16[2,2,65536]{2,1,0:T(2,128)(2,1)} %reshape.420), calls=%async_computation.1 | async-start | bytes 1048576 | tf_op jit(solution)/shard_map/all_to_all | solution.py:114
  25.6 31.9 %copy-start.25 = (f32[8]{0:T(128)}, f32[8]{0:T(128)S(1)}, u32[]{:S(2)}) copy-start(f32[8]{0:T(128)S(1)} %dynamic_slice.111) | copy-start | bytes 100
  25.6 31.8 %copy-start.27 = (f32[8]{0:T(128)}, f32[8]{0:T(128)S(1)}, u32[]{:S(2)}) copy-start(f32[8]{0:T(128)S(1)} %fusion.50) | copy-start | bytes 100
  43.3 7.0 %all-to-all-start.2 = ((bf16[2,2,65536]{2,1,0:T(2,128)(2,1)}), bf16[2,2,65536]{2,1,0:T(2,128)(2,1)}, u32[]{:S(2)}, u32[]{:S(2)}) async-start(bf16[2,2,65536]{2,1,0:T(2,128)(2,1)} %reshape.422), calls=%async_computation.2 | async-start | bytes 1048576 | tf_op jit(solution)/shard_map/all_to_all | solution.py:115
  50.4 7.1 %all-to-all-start = ((f32[1,256,16]{1,0,2:T(1,128)}), f32[1,256,16]{1,0,2:T(1,128)S(1)}, u32[]{:S(2)}, u32[]{:S(2)}) async-start(f32[1,256,16]{1,0,2:T(1,128)} %copy.56), calls=%async_computation | async-start | bytes 32768 | tf_op jit(solution)/shard_map/all_to_all | solution.py:117
  53.6 203.8 %reduce-scatter.3.cloned.1.call-start = ((), (), s32[]{:S(2)}) async-start(), calls=%async_computation.7 | async-start | bytes 786432 | tf_op jit(solution)/shard_map/reduce_scatter | solution.py:151
  82.4 9.5 %copy-start.7 = (f32[256]{0:T(256)}, f32[256]{0:T(256)S(1)}, u32[]{:S(2)}) copy-start(f32[256]{0:T(256)S(1)} %get-tuple-element.920) | copy-start | bytes 3076 | tf_op jit(solution)/shard_map/transpose(jvp())/while
  83.5 8.5 %copy-start.11 = (f32[8]{0:T(128)}, f32[8]{0:T(128)S(1)}, u32[]{:S(2)}) copy-start(f32[8]{0:T(128)S(1)} %get-tuple-element.913) | copy-start | bytes 100 | tf_op jit(solution)/shard_map/transpose(jvp())/while
  86.1 4.1 %copy-start.1 = (f32[256,256]{1,0:T(8,128)}, f32[256,256]{1,0:T(8,128)S(1)}, u32[]{:S(2)}) copy-start(f32[256,256]{1,0:T(8,128)S(1)} %fusion.108) | copy-start | bytes 786436 | tf_op jit(solution)/shard_map/transpose(jvp())/while
  99.4 4.7 %copy-start.12 = (f32[2,256,8]{1,2,0:T(8,128)S(1)}, f32[2,256,8]{1,2,0:T(8,128)}, u32[]{:S(2)}) copy-start(f32[2,256,8]{1,2,0:T(8,128)} %get-tuple-element.997) | copy-start | bytes 49156 | tf_op jit(solution)/shard_map/transpose(jvp())/while
  99.4 5.3 %copy-start.19 = (s32[2,256]{1,0:T(2,128)S(1)}, s32[2,256]{1,0:T(2,128)}, u32[]{:S(2)}) copy-start(s32[2,256]{1,0:T(2,128)} %copy-done.18) | copy-start | bytes 6148 | tf_op jit(solution)/shard_map/transpose(jvp())/while
  99.4 5.3 %copy-start.35 = (s32[2]{0:T(128)S(1)}, s32[2]{0:T(128)}, u32[]{:S(2)}) copy-start(s32[2]{0:T(128)} %copy-done.34) | copy-start | bytes 28 | tf_op jit(solution)/shard_map/transpose(jvp())/while
  100.8 3.9 %copy-start.3 = (f32[2,256,256]{2,1,0:T(8,128)S(1)}, f32[2,256,256]{2,1,0:T(8,128)}, u32[]{:S(2)}) copy-start(f32[2,256,256]{2,1,0:T(8,128)} %copy-done.2) | copy-start | bytes 1572868 | tf_op jit(solution)/shard_map/transpose(jvp())/while
  113.2 9.5 %copy-start.7 = (f32[256]{0:T(256)}, f32[256]{0:T(256)S(1)}, u32[]{:S(2)}) copy-start(f32[256]{0:T(256)S(1)} %get-tuple-element.920) | copy-start | bytes 3076 | tf_op jit(solution)/shard_map/transpose(jvp())/while
  114.3 8.4 %copy-start.11 = (f32[8]{0:T(128)}, f32[8]{0:T(128)S(1)}, u32[]{:S(2)}) copy-start(f32[8]{0:T(128)S(1)} %get-tuple-element.913) | copy-start | bytes 100 | tf_op jit(solution)/shard_map/transpose(jvp())/while
  116.9 4.1 %copy-start.1 = (f32[256,256]{1,0:T(8,128)}, f32[256,256]{1,0:T(8,128)S(1)}, u32[]{:S(2)}) copy-start(f32[256,256]{1,0:T(8,128)S(1)} %fusion.108) | copy-start | bytes 786436 | tf_op jit(solution)/shard_map/transpose(jvp())/while
  130.1 4.7 %copy-start.12 = (f32[2,256,8]{1,2,0:T(8,128)S(1)}, f32[2,256,8]{1,2,0:T(8,128)}, u32[]{:S(2)}) copy-start(f32[2,256,8]{1,2,0:T(8,128)} %get-tuple-element.997) | copy-start | bytes 49156 | tf_op jit(solution)/shard_map/transpose(jvp())/while
  130.1 5.3 %copy-start.19 = (s32[2,256]{1,0:T(2,128)S(1)}, s32[2,256]{1,0:T(2,128)}, u32[]{:S(2)}) copy-start(s32[2,256]{1,0:T(2,128)} %copy-done.18) | copy-start | bytes 6148 | tf_op jit(solution)/shard_map/transpose(jvp())/while
  130.2 5.3 %copy-start.35 = (s32[2]{0:T(128)S(1)}, s32[2]{0:T(128)}, u32[]{:S(2)}) copy-start(s32[2]{0:T(128)} %copy-done.34) | copy-start | bytes 28 | tf_op jit(solution)/shard_map/transpose(jvp())/while
  135.6 4.2 %copy-start.23 = (f32[8]{0:T(128)S(1)}, f32[8]{0:T(128)}, u32[]{:S(2)}) copy-start(f32[8]{0:T(128)} %get-tuple-element.453) | copy-start | bytes 100
  135.6 4.4 %copy-start.31 = (f32[16]{0:T(128)S(1)}, f32[16]{0:T(128)}, u32[]{:S(2)}) copy-start(f32[16]{0:T(128)} %param.19) | copy-start | bytes 196
  135.6 107.7 %copy-start.4 = (bf16[2,256,8,64]{1,3,2,0:T(8,128)(2,1)S(1)}, bf16[2,256,8,64]{1,3,2,0:T(8,128)(2,1)}, u32[]{:S(2)}) copy-start(bf16[2,256,8,64]{1,3,2,0:T(8,128)(2,1)} %get-tuple-element.448) | copy-start | bytes 1572868
  135.6 123.4 %reduce-scatter.5.cloned.1.call-start = ((), (), s32[]{:S(2)}) async-start(), calls=%async_computation.8 | async-start | bytes 786432 | tf_op jit(solution)/shard_map/reduce_scatter | solution.py:152
  140.1 109.4 %all-to-all-start.4 = ((f32[2,1,2048]{2,1,0:T(1,128)}), f32[2,1,2048]{2,1,0:T(1,128)S(1)}, u32[]{:S(2)}, u32[]{:S(2)}) async-start(f32[2,1,2048]{2,1,0:T(1,128)} %reshape.426), calls=%async_computation.6 | async-start | bytes 32768 | tf_op jit(solution)/shard_map/all_to_all | solution.py:149
  249.5 6.0 %all-to-all-start.3 = ((bf16[2,2,65536]{2,1,0:T(2,128)(2,1)}), bf16[2,2,65536]{2,1,0:T(2,128)(2,1)S(1)}, u32[]{:S(2)}, u32[]{:S(2)}) async-start(bf16[2,2,65536]{2,1,0:T(2,128)(2,1)} %reshape.424), calls=%async_computation.3 | async-start | bytes 1048576 | tf_op jit(solution)/shard_map/all_to_all | solution.py:142
  (29 other events, 42.8 us)
Sparse Core Ops, SparseCore 0:
  135.7 16.2 reduce-scatter.2
  155.1 17.3 reduce-scatter.4
where the time goes:
time: 269 us; the launch traced here: 267 us
  blocking collectives  106 us (39%)
  other arithmetic  44.1 us (16%)
  local copies, waits for them, and re-layouts  38.4 us (14%)
  matrix products  32.5 us (12%)
  starting transfers between devices  26 us (10%)
  between operations  14.4 us (5%)
  loops' own time  5.8 us (2%)
    psum x1, blocking collectives, on_device(): lax.psum((partial_sums[0], partial_sums[1], partial_sums[2]), ('dp', 'ctx'))  99.9 us
    unnamed x54, local copies, waits for them, and re-layouts  17.9 us
    dot_general x4, matrix products, advance(): result = jnp.einsum('ijh,jhp->ihp', mixing, in_block, precision=highest)  15.2 us
    unnamed x7, other arithmetic  13.7 us
    all_to_all x1, starting transfers between devices, on_device(): lax.all_to_all(head_inputs, 'ctx', split_axis=2, concat_axis=1, tiled=True)  10.5 us
    another operation x17, other arithmetic  9.32 us
    dot_general x6, matrix products, advance(): jnp.einsum('jh,jhp,jn->hpn', tail, in_block, write_block, precision=highest)  7.06 us
    dot_general x6, matrix products, advance(): jnp.einsum('in,hpn->ihp', read_block, state, precision=highest)  6.04 us
  transfers between devices with their start and end apart: 7, of which 0 were waited for; matrix products, arithmetic and copies ran while one was open for 12% of the time, Pallas kernels for 0%

commit v1 on v0

v1 whole, which is shorter than its diff:
```python
import jax
import jax.numpy as jnp
from jax import lax
from jax.experimental import pallas as pl
from jax.experimental.pallas import tpu as pltpu
from jax.sharding import PartitionSpec as P

HEADS = 16
HEAD_DIM = 64
STATE = 256
BLOCK = 256
WIDTH = HEADS * HEAD_DIM
HALF = BLOCK // 2
PAIR = 2 * HEAD_DIM
F32 = jnp.float32
BF16 = jnp.bfloat16
NEG = -1e30

NN = (((1,), (0,)), ((), ()))
NT = (((1,), (1,)), ((), ()))


def dot(a, b, dims=NN):
    return lax.dot_general(a, b, dims, preferred_element_type=F32)


def split2(v):
    hi = v.astype(BF16)
    return hi, (v - hi.astype(F32)).astype(BF16)


def split3(v):
    hi = v.astype(BF16)
    rest = v - hi.astype(F32)
    mid = rest.astype(BF16)
    return hi, mid, (rest - mid.astype(F32)).astype(BF16)


def softplus(z):
    u = jnp.exp(-jnp.abs(z))
    series = u * (1.0 - u * (0.5 - u * (1.0 / 3.0 - u * 0.25)))
    return jnp.maximum(z, 0.0) + jnp.where(u < 0.01, series, jnp.log(1.0 + u))


def head_rows():
    lane = lax.broadcasted_iota(jnp.int32, (HEADS, WIDTH), 1)
    head = lax.broadcasted_iota(jnp.int32, (HEADS, WIDTH), 0)
    return (lax.shift_right_logical(lane, 6) == head).astype(BF16)


def expand(v, rows):
    hi, mid, lo = split3(v)
    return dot(hi, rows) + dot(mid, rows) + dot(lo, rows)


def head_sums(v, rows):
    hi, mid, lo = split3(v)
    return dot(hi, rows, NT) + dot(mid, rows, NT) + dot(lo, rows, NT)


def tri_ones(lower):
    r = lax.broadcasted_iota(jnp.int32, (BLOCK, BLOCK), 0)
    c = lax.broadcasted_iota(jnp.int32, (BLOCK, BLOCK), 1)
    return ((r >= c) if lower else (r <= c)).astype(BF16)


def transpose_heads(v):
    wide = jnp.concatenate([v, jnp.zeros((BLOCK, 128 - HEADS), F32)], axis=1)
    return wide.T[0:HEADS]


def columns(row):
    return jnp.broadcast_to(row, (128, BLOCK)).T


def outgoing_kernel(
    doc_ref, raw_ref, bias_ref, lr_ref, x_ref, c_ref, w_ref, r_ref,
    send_ref, f_ref, s_ref, cum_ref, cumt_ref,
):
    first = lax.axis_index("ctx") == 0
    z = raw_ref[0] + bias_ref[...]
    s = softplus(z)
    rate = s * (-jnp.exp(lr_ref[...]))
    tri = tri_ones(True)
    hi, mid, lo = split3(rate)
    cum = dot(tri, hi) + dot(tri, mid) + dot(tri, lo)
    s_ref[...] = s
    cum_ref[...] = cum
    cumt_ref[...] = transpose_heads(cum)
    doc = doc_ref[...].astype(F32)
    doc_col = columns(doc)[:, 0:HEADS]
    edge = jnp.where(first, doc[:, BLOCK - 1 :], doc[:, 0:1])
    arg = jnp.where(first, cum[BLOCK - 1 :] - cum, cum)
    gain = jnp.where(first, s, jnp.ones_like(s))
    f = jnp.where(doc_col == edge, jnp.exp(arg) * gain, 0.0)
    f_ref[...] = f
    wide = expand(f, head_rows())
    v = jnp.where(first, x_ref[0], c_ref[0]).astype(F32) * wide
    k = jnp.where(first, w_ref[0], r_ref[0]).T
    hi, lo = split2(v)
    send_ref[0:STATE] = dot(k, hi) + dot(k, lo)
    send_ref[STATE:] = jnp.broadcast_to(edge, (8, WIDTH))


def intra_kernel(
    doc_ref, s_ref, cum_ref, cumt_ref, x_ref, c_ref, w_ref, r_ref,
    dx_ref, dw_ref, dr_ref, col_ref,
    mask_ref, p_ref, dp_ref, colt_ref,
):
    doc = doc_ref[...].astype(F32)
    doc_col = columns(doc)
    for t in range(2):
        span = slice(t * HALF, (t + 1) * HALF)
        j = lax.broadcasted_iota(jnp.int32, (BLOCK, HALF), 0)
        i = lax.broadcasted_iota(jnp.int32, (BLOCK, HALF), 1) + t * HALF
        ok = (i >= j) & (doc_col == doc[:, span])
        mask_ref[:, span] = jnp.where(ok, 0.0, NEG)
    p_ref[...] = dot(w_ref[0], r_ref[0], NT)
    dp_ref[...] = jnp.zeros((BLOCK, BLOCK), F32)
    colj = cum_ref[...] - jnp.log(s_ref[...])
    lane = lax.broadcasted_iota(jnp.int32, (BLOCK, PAIR), 1)
    for pair in range(HEADS // 2):
        lanes = slice(pair * PAIR, (pair + 1) * PAIR)
        xp, cp = x_ref[0, :, lanes], c_ref[0, :, lanes]
        top = bottom = None
        for odd in range(2):
            h = 2 * pair + odd
            ch = jnp.where((lane < HEAD_DIM) != bool(odd), cp, jnp.zeros_like(cp))
            row = cumt_ref[h : h + 1, :]
            col = colj[:, h : h + 1]

            def tile(js, isl):
                g = dot(xp[js], ch[isl], NT)
                ell = jnp.exp((row[:, isl] - col[js]) + mask_ref[js, isl])
                m = ell * p_ref[js, isl]
                dp_ref[js, isl] += ell * g
                hi, lo = split2(m)
                return dot(hi, ch[isl]) + dot(lo, ch[isl]), jnp.sum(m * g, axis=0, keepdims=True)

            d0, e0 = tile(slice(0, HALF), slice(0, BLOCK))
            d1, e1 = tile(slice(HALF, BLOCK), slice(HALF, BLOCK))
            colt_ref[h : h + 1, 0:HALF] = e0[:, 0:HALF]
            colt_ref[h : h + 1, HALF:] = e0[:, HALF:] + e1
            top = d0 if top is None else top + d0
            bottom = d1 if bottom is None else bottom + d1
        dx_ref[0:HALF, lanes] = top
        dx_ref[HALF:, lanes] = bottom
    dp = dp_ref[...]
    hi, lo = split2(dp)
    dw_ref[...] = dot(hi, r_ref[0]) + dot(lo, r_ref[0])
    hi, lo = split2(dp.T)
    dr_ref[...] = dot(hi, w_ref[0]) + dot(lo, w_ref[0])
    col_ref[...] = colt_ref[...].T[:, 0:HEADS]


def final_kernel(
    got_ref, doc_ref, raw_ref, bias_ref, lr_ref, skip_ref, f_ref, s_ref,
    x_ref, c_ref, w_ref, r_ref, dxi_ref, dwi_ref, dri_ref, col_ref,
    dx_ref, dw_ref, dr_ref, dstep_ref, sums_ref,
):
    first = lax.axis_index("ctx") == 0
    doc = doc_ref[...].astype(F32)
    edge = jnp.where(first, doc[:, BLOCK - 1 :], doc[:, 0:1])
    joined = (got_ref[STATE : STATE + 1, 0:1] == edge).astype(F32)
    rows = head_rows()
    f = f_ref[...] * joined
    s = s_ref[...]
    wide = expand(f, rows)
    x, c = x_ref[0].astype(F32), c_ref[0].astype(F32)
    v = jnp.where(first, x, c)
    k = jnp.where(first, w_ref[0], r_ref[0])
    t_hi, t_lo = split2(got_ref[0:STATE])
    zs = (dot(k, t_hi) + dot(k, t_lo)) * wide
    vf_hi, vf_lo = split2(v * wide)
    dk = dot(vf_hi, t_hi, NT) + dot(vf_lo, t_hi, NT) + dot(vf_hi, t_lo, NT)
    zero = jnp.zeros_like(dk)
    dw_ref[0] = (dwi_ref[...] + jnp.where(first, dk, zero)).astype(BF16)
    dr_ref[0] = (dri_ref[...] + jnp.where(first, zero, dk)).astype(BF16)
    u = head_sums(v * zs, rows)
    dxi = dxi_ref[...]
    q = head_sums(x * dxi, rows)
    gains = expand(jnp.broadcast_to(skip_ref[...], (8, HEADS)), rows)[0:1]
    dx = dxi + jnp.where(first, zs, 0.0) + gains * c
    dx_ref[0] = dx.astype(BF16)
    q = q + jnp.where(first, u, 0.0)
    da = col_ref[...] - q + jnp.where(first, 0.0, u)
    hi, mid, lo = split3(da)
    tri = tri_ones(False)
    drate = dot(tri, hi) + dot(tri, mid) + dot(tri, lo)
    drate = drate + jnp.where(first, jnp.sum(u, axis=0, keepdims=True), 0.0)
    ell = jnp.exp(lr_ref[...])
    z = raw_ref[0] + bias_ref[...]
    dstep = (q / s - drate * ell) / (1.0 + jnp.exp(-z))
    dstep_ref[0] = dstep
    sum_bias = jnp.sum(dstep, axis=0, keepdims=True)
    sum_rate = jnp.sum(drate * (s * -ell), axis=0, keepdims=True)
    cx = jnp.sum(c * x, axis=0, keepdims=True)
    sum_skip = head_sums(jnp.broadcast_to(cx, (8, WIDTH)), rows)[0:1]
    pad = jnp.zeros((1, 128 - 3 * HEADS), F32)
    sums_ref[...] = jnp.concatenate([sum_rate, sum_bias, sum_skip, pad], axis=1)


def call(kernel, outs, scratch=(), flops=0, bytes_accessed=0):
    return pl.pallas_call(
        kernel,
        out_shape=outs,
        scratch_shapes=list(scratch),
        compiler_params=pltpu.CompilerParams(vmem_limit_bytes=40 << 20),
        cost_estimate=pl.CostEstimate(
            flops=flops, bytes_accessed=bytes_accessed, transcendentals=0
        ),
    )


def shape(dims, dtype=F32):
    return jax.ShapeDtypeStruct(dims, dtype)


def mesh_sum(sums, devices):
    sums = lax.psum(sums, "ctx")
    everyone = jnp.broadcast_to(sums, (devices, 128))
    everyone = lax.all_to_all(everyone, "dp", split_axis=0, concat_axis=0, tiled=True)
    return jnp.sum(everyone, axis=0)


def on_device(x, c, w, r, raw, doc, log_rate, step_bias, skip_gain):
    lr, bias, skip = log_rate[None], step_bias[None], skip_gain[None]
    per_head = shape((BLOCK, HEADS))
    send, f, s, cum, cumt = call(
        outgoing_kernel,
        (shape((STATE + 8, WIDTH)), per_head, per_head, per_head, shape((HEADS, BLOCK))),
        flops=300_000_000,
        bytes_accessed=3 << 20,
    )(doc, raw, bias, lr, x, c, w, r)
    got = lax.ppermute(send, "ctx", [(0, 1), (1, 0)])
    square = shape((BLOCK, STATE))
    dxi, dwi, dri, col = call(
        intra_kernel,
        (shape((BLOCK, WIDTH)), square, square, per_head),
        scratch=(
            pltpu.VMEM((BLOCK, BLOCK), F32),
            pltpu.VMEM((BLOCK, BLOCK), F32),
            pltpu.VMEM((BLOCK, BLOCK), F32),
            pltpu.VMEM((HEADS, BLOCK), F32),
        ),
        flops=2_000_000_000,
        bytes_accessed=4 << 20,
    )(doc, s, cum, cumt, x, c, w, r)
    grad_x, grad_w, grad_r, grad_step, sums = call(
        final_kernel,
        (
            shape((1, BLOCK, WIDTH), BF16),
            shape((1, BLOCK, STATE), BF16),
            shape((1, BLOCK, STATE), BF16),
            shape((1, BLOCK, HEADS)),
            shape((1, 128)),
        ),
        flops=1_000_000_000,
        bytes_accessed=5 << 20,
    )(got, doc, raw, bias, lr, skip, f, s, x, c, w, r, dxi, dwi, dri, col)
    total = mesh_sum(sums, lax.axis_size("dp"))
    return (
        grad_x, grad_w, grad_r, grad_step,
        total[0:HEADS], total[HEADS : 2 * HEADS], total[2 * HEADS : 3 * HEADS],
    )


def solution(mesh):
    split = P("dp", "ctx", None)
    return jax.shard_map(
        on_device,
        mesh=mesh,
        in_specs=(split, split, split, split, split, P("dp", "ctx"), P(), P(), P()),
        out_specs=(split, split, split, split, P(), P(), P()),
        check_vma=False,
    )
```

time: 269 us -> 57.4 us (0.21)
  blocking collectives: 106 us -> 2.45 us
  other arithmetic: 44.1 us -> 0.05 us
  matrix products: 32.5 us -> 0 us
  local copies, waits for them, and re-layouts: 38.4 us -> 8.74 us
  between operations: 14.4 us -> 0.73 us
  waiting for transfers between devices: 0.51 us -> 11.4 us
  Pallas kernels: 0 us -> 7.92 us
  loops' own time: 5.8 us -> 0 us
    psum x1, blocking collectives: 99.9 us -> 2.45 us  [mesh_sum(): sums = lax.psum(sums, 'ctx')]
    dot_general x22 -> x0, matrix products: 32.5 us -> none  [the longest x4 15.2 us: advance(): result = jnp.einsum('ijh,jhp->ihp', mixing, in_block, precision=highest)]
    unnamed x7 -> x0, other arithmetic: 13.7 us -> none
    all_to_all x5 -> x1, waiting for transfers between devices: 0.01 us -> 11.4 us  [mesh_sum(): lax.all_to_all(everyone, 'dp', split_axis=0, concat_axis=0, tiled=True)]
    another operation x19 -> x0, other arithmetic: 10.5 us -> none
    unnamed x54 -> x24, local copies, waits for them, and re-layouts: 17.9 us -> 7.42 us
    convert_element_type x10 -> x0, other arithmetic: 9.31 us -> none  [the longest x4 3.84 us: advance(): (doc_block == end_doc).astype(jnp.float32)[:, None]]
    ppermute x0 -> x1, starting transfers between devices: none -> 8.78 us  [on_device(): got = lax.ppermute(send, 'ctx', [(0, 1), (1, 0)])]
  transfers between devices with their start and end apart: 7 -> 2, of which waited for: 0 -> 1; matrix products, arithmetic and copies ran while one was open for 12% -> 1% of each run, Pallas kernels for 0% -> 5%
where the time goes in v1:
time: 57.4 us; the launch traced here: 57.1 us
  starting transfers between devices  25.8 us (45%)
  waiting for transfers between devices  11.4 us (20%)
  local copies, waits for them, and re-layouts  8.74 us (15%)
  Pallas kernels  7.92 us (14%)
  blocking collectives  2.45 us (4%)
  between operations  0.73 us (1%)
    all_to_all x1, starting transfers between devices, mesh_sum(): lax.all_to_all(everyone, 'dp', split_axis=0, concat_axis=0, tiled=True)  17 us
    all_to_all x1, waiting for transfers between devices, mesh_sum(): lax.all_to_all(everyone, 'dp', split_axis=0, concat_axis=0, tiled=True)  11.4 us
    ppermute x1, starting transfers between devices, on_device(): got = lax.ppermute(send, 'ctx', [(0, 1), (1, 0)])  8.78 us
    unnamed x24, local copies, waits for them, and re-layouts  7.42 us
    pallas_call x1, Pallas kernels, on_device(): call(final_kernel, (shape((1, BLOCK, WIDTH), BF16), shape((1, BLOCK, STAT...  3.9 us
    pallas_call x1, Pallas kernels, on_device(): call(intra_kernel, (shape((BLOCK, WIDTH)), square, square, per_head), scr...  2.7 us
    psum x1, blocking collectives, mesh_sum(): sums = lax.psum(sums, 'ctx')  2.45 us
    pallas_call x1, Pallas kernels, on_device(): call(outgoing_kernel, (shape((STATE + 8, WIDTH)), per_head, per_head, per...  1.32 us
  transfers between devices with their start and end apart: 2, of which 1 were waited for; matrix products, arithmetic and copies ran while one was open for 1% of the time, Pallas kernels for 5%

profile of v1, /device:TPU:1, one launch (start us, length us, event | category | flops | bytes accessed | tf_op | source)
XLA Modules:
  0.0 57.1 jit_solution(12752163310301998442)
XLA Ops:
  0.6 0.0 copy-start.6
  0.6 0.9 %copy.22.raw_ref = f32[1,256,16]{2,1,0:T(8,128)S(1)} copy(f32[1,256,16]{1,2,0:T(8,128)} %param.13) | data formatting | bytes 32768 | tf_op args[4]
  1.5 0.0 copy-start
  1.5 1.0 %copy-done = bf16[1,256,1024]{2,1,0:T(8,128)(2,1)S(1)} copy-done((bf16[1,256,1024]{2,1,0:T(8,128)(2,1)S(1)}, bf16[1,256,1024]{2,1,0:T(8,128)(2,1)}, u32[]{:S(2)}) %copy-start) | copy-done | bytes 524312
  2.5 0.0 copy-start.2
  2.5 1.0 %copy-done.2 = bf16[1,256,1024]{2,1,0:T(8,128)(2,1)S(1)} copy-done((bf16[1,256,1024]{2,1,0:T(8,128)(2,1)S(1)}, bf16[1,256,1024]{2,1,0:T(8,128)(2,1)}, u32[]{:S(2)}) %copy-start.2) | copy-done | bytes 524312
  3.6 0.0 copy-start.4
  3.6 0.9 %copy-done.4 = bf16[1,256,256]{2,1,0:T(8,128)(2,1)S(1)} copy-done((bf16[1,256,256]{2,1,0:T(8,128)(2,1)S(1)}, bf16[1,256,256]{2,1,0:T(8,128)(2,1)}, u32[]{:S(2)}) %copy-start.4) | copy-done | bytes 131096
  4.5 0.0 copy-start.5
  4.5 0.9 %copy-done.5 = bf16[1,256,256]{2,1,0:T(8,128)(2,1)S(1)} copy-done((bf16[1,256,256]{2,1,0:T(8,128)(2,1)S(1)}, bf16[1,256,256]{2,1,0:T(8,128)(2,1)}, u32[]{:S(2)}) %copy-start.5) | copy-done | bytes 131096
  5.4 0.0 copy-start.7
  5.4 0.7 %copy-done.7 = s32[1,256]{1,0:T(1,128)S(1)} copy-done((s32[1,256]{1,0:T(1,128)S(1)}, s32[1,256]{1,0:T(1,128)}, u32[]{:S(2)}) %copy-start.7) | copy-done | bytes 1048
  6.1 0.0 copy-start.8
  6.1 0.7 %copy-done.8 = f32[16]{0:T(128)S(1)} copy-done((f32[16]{0:T(128)S(1)}, f32[16]{0:T(128)}, u32[]{:S(2)}) %copy-start.8) | copy-done | bytes 88
  6.7 0.0 copy-start.9
  6.7 0.7 %copy-done.9 = f32[16]{0:T(128)S(1)} copy-done((f32[16]{0:T(128)S(1)}, f32[16]{0:T(128)}, u32[]{:S(2)}) %copy-start.9) | copy-done | bytes 88
  7.4 1.3 %shard_map.144 = (f32[264,1024]{1,0:T(8,128)S(1)}, f32[256,16]{1,0:T(8,128)S(1)}, f32[256,16]{1,0:T(8,128)S(1)}, f32[256,16]{1,0:T(8,128)S(1)}, f32[16,256]{1,0:T(8,128)S(1)}) custom-call(s32[1,256]{1,0:T(1,128)S(1)} %copy-done.7, f32[1,256,16]{2,1,0:T(8,128)S(1)} %copy.22.raw_ref, f32[1,16]{1,0:T(1,128)S(1)} %bitcast.5, f32[1,16]{1,0:T(1,128)S(1)} %bitcast.7, ...), custom_call_target="tpu_custom_call" | custom-call | flops 300000000 | bytes 3145728 | tf_op jit(solution)/shard_map/pallas_call | solution.py:229
  8.7 8.8 %collective-permute-start = (f32[264,1024]{1,0:T(8,128)S(1)}, f32[264,1024]{1,0:T(8,128)S(1)}, u32[]{:S(2)}, u32[]{:S(2)}) collective-permute-start(f32[264,1024]{1,0:T(8,128)S(1)} %get-tuple-element.21), channel_id=1, source_target_pairs={{0,1},{1,0},{2,3},{3,2},{4,5},{5,4},{6,7},{7,6},{8,9},{9,8},{10,11... | collective-permute-start | bytes 3244040 | tf_op jit(solution)/shard_map/ppermute | solution.py:235
  17.5 0.0 copy-done.6
  17.5 0.0 copy-done.1
  17.5 0.0 copy-done.3
  17.5 0.0 copy-start.10
  17.5 2.7 %shard_map.145 = (f32[256,1024]{1,0:T(8,128)S(1)}, f32[256,256]{1,0:T(8,128)S(1)}, f32[256,256]{1,0:T(8,128)S(1)}, f32[256,16]{1,0:T(8,128)S(1)}) custom-call(s32[1,256]{1,0:T(1,128)S(1)} %copy-done.7, f32[256,16]{1,0:T(8,128)S(1)} %get-tuple-element.23.s_ref, f32[256,16]{1,0:T(8,128)S(1)} %get-tuple-element.24.cum_ref, ...), custom_call_target="tpu_custom_call" | custom-call | flops 2000000000 | bytes 4194304 | tf_op jit(solution)/shard_map/pallas_call | solution.py:237
  20.2 0.0 collective-permute-done.got_ref
  20.3 0.0 copy-done.10
  20.3 3.9 %shard_map.146 = (bf16[1,256,1024]{2,1,0:T(8,128)(2,1)}, bf16[1,256,256]{2,1,0:T(8,128)(2,1)}, bf16[1,256,256]{2,1,0:T(8,128)(2,1)}, f32[1,256,16]{2,1,0:T(8,128)S(1)}, f32[1,128]{1,0:T(1,128)S(1)}) custom-call(f32[264,1024]{1,0:T(8,128)S(1)} %collective-permute-done.got_ref, s32[1,256]{1,0:T(1,128)S(1)} %copy-done.7, f32[1,256,16]{2,1,0:T(8,128)S(1)} %copy.22.raw_ref, ...), custom_call_target="tpu_custom_call" | custom-call | flops 1000000000 | bytes 5242880 | tf_op jit(solution)/shard_map/pallas_call | solution.py:249
  24.2 2.5 %psum.10 = f32[128]{0:T(128)S(1)} all-reduce(f32[128]{0:T(128)S(1)} %bitcast.10), channel_id=1, replica_groups=mesh['dp'=256,'ctx'=2] {'ctx'}, use_global_device_ids=true, to_apply=%region_0.0 | all-reduce | flops 128 | bytes 1024 | tf_op jit(solution)/shard_map/psum | solution.py:220
  26.6 0.7 %broadcast_in_dim.17 = f32[256,1,128]{2,1,0:T(1,128)} broadcast(f32[128]{0:T(128)S(1)} %psum.10), dimensions={2} | broadcast | bytes 131584 | tf_op jit(solution)/shard_map/broadcast_in_dim | solution.py:221
  27.3 17.0 %all-to-all-start = ((f32[256,1,128]{2,1,0:T(1,128)}), f32[256,1,128]{2,1,0:T(1,128)S(1)}, u32[]{:S(2)}, u32[]{:S(2)}) async-start(f32[256,1,128]{2,1,0:T(1,128)} %broadcast_in_dim.17), calls=%async_computation | async-start | bytes 262144 | tf_op jit(solution)/shard_map/all_to_all | solution.py:222
  44.3 0.7 %copy.25 = f32[1,256,16]{1,2,0:T(8,128)} copy(f32[1,256,16]{2,1,0:T(8,128)S(1)} %get-tuple-element.52) | data formatting | bytes 32768
  45.0 11.4 %all-to-all-done = f32[256,1,128]{2,1,0:T(1,128)S(1)} async-done(((f32[256,1,128]{2,1,0:T(1,128)}), f32[256,1,128]{2,1,0:T(1,128)S(1)}, u32[]{:S(2)}, u32[]{:S(2)}) %all-to-all-start) | async-done | bytes 131104 | tf_op jit(solution)/shard_map/all_to_all | solution.py:222
  56.5 0.6 %fusion = (f32[16]{0:T(128)}, f32[16]{0:T(128)}, f32[16]{0:T(128)}) fusion(f32[128]{0:T(128)S(1)} %reduce_sum.9), kind=kLoop, calls=%fused_computation | loop fusion | bytes 384 | tf_op jit(solution)/shard_map/slice | solution.py:264
  (3 shorter events, 0.1 us)
Async XLA Ops:
  0.6 16.9 %copy-start.6 = (bf16[1,256,256]{2,1,0:T(8,128)(2,1)S(1)}, bf16[1,256,256]{2,1,0:T(8,128)(2,1)}, u32[]{:S(2)}) copy-start(bf16[1,256,256]{2,1,0:T(8,128)(2,1)} %r_ref.5) | copy-start | bytes 393220
  1.5 1.0 %copy-start = (bf16[1,256,1024]{2,1,0:T(8,128)(2,1)S(1)}, bf16[1,256,1024]{2,1,0:T(8,128)(2,1)}, u32[]{:S(2)}) copy-start(bf16[1,256,1024]{2,1,0:T(8,128)(2,1)} %x_ref.5) | copy-start | bytes 1572868
  2.5 1.0 %copy-start.2 = (bf16[1,256,1024]{2,1,0:T(8,128)(2,1)S(1)}, bf16[1,256,1024]{2,1,0:T(8,128)(2,1)}, u32[]{:S(2)}) copy-start(bf16[1,256,1024]{2,1,0:T(8,128)(2,1)} %c_ref.5) | copy-start | bytes 1572868
  3.6 0.9 %copy-start.4 = (bf16[1,256,256]{2,1,0:T(8,128)(2,1)S(1)}, bf16[1,256,256]{2,1,0:T(8,128)(2,1)}, u32[]{:S(2)}) copy-start(bf16[1,256,256]{2,1,0:T(8,128)(2,1)} %w_ref.5) | copy-start | bytes 393220
  4.5 0.9 %copy-start.5 = (bf16[1,256,256]{2,1,0:T(8,128)(2,1)S(1)}, bf16[1,256,256]{2,1,0:T(8,128)(2,1)}, u32[]{:S(2)}) copy-start(bf16[1,256,256]{2,1,0:T(8,128)(2,1)} %r_ref.5) | copy-start | bytes 393220
  5.4 0.7 %copy-start.7 = (s32[1,256]{1,0:T(1,128)S(1)}, s32[1,256]{1,0:T(1,128)}, u32[]{:S(2)}) copy-start(s32[1,256]{1,0:T(1,128)} %doc_ref.5) | copy-start | bytes 3076
  6.1 0.7 %copy-start.8 = (f32[16]{0:T(128)S(1)}, f32[16]{0:T(128)}, u32[]{:S(2)}) copy-start(f32[16]{0:T(128)} %param.16) | copy-start | bytes 196
  6.7 0.7 %copy-start.9 = (f32[16]{0:T(128)S(1)}, f32[16]{0:T(128)}, u32[]{:S(2)}) copy-start(f32[16]{0:T(128)} %param.15) | copy-start | bytes 196
  7.4 10.1 %copy-start.1 = (bf16[1,256,1024]{2,1,0:T(8,128)(2,1)S(1)}, bf16[1,256,1024]{2,1,0:T(8,128)(2,1)}, u32[]{:S(2)}) copy-start(bf16[1,256,1024]{2,1,0:T(8,128)(2,1)} %x_ref.5) | copy-start | bytes 1572868
  7.4 10.1 %copy-start.3 = (bf16[1,256,1024]{2,1,0:T(8,128)(2,1)S(1)}, bf16[1,256,1024]{2,1,0:T(8,128)(2,1)}, u32[]{:S(2)}) copy-start(bf16[1,256,1024]{2,1,0:T(8,128)(2,1)} %c_ref.5) | copy-start | bytes 1572868
  8.7 11.5 %collective-permute-start = (f32[264,1024]{1,0:T(8,128)S(1)}, f32[264,1024]{1,0:T(8,128)S(1)}, u32[]{:S(2)}, u32[]{:S(2)}) collective-permute-start(f32[264,1024]{1,0:T(8,128)S(1)} %get-tuple-element.21), channel_id=1, source_target_pairs={{0,1},{1,0},{2,3},{3,2},{4,5},{5,4},{6,7},{7,6},{8,9},{9,8},{10,11... | collective-permute-start | bytes 3244040 | tf_op jit(solution)/shard_map/ppermute | solution.py:235
  17.5 2.7 %copy-start.10 = (f32[16]{0:T(128)S(1)}, f32[16]{0:T(128)}, u32[]{:S(2)}) copy-start(f32[16]{0:T(128)} %param.17) | copy-start | bytes 196
  27.3 29.1 %all-to-all-start = ((f32[256,1,128]{2,1,0:T(1,128)}), f32[256,1,128]{2,1,0:T(1,128)S(1)}, u32[]{:S(2)}, u32[]{:S(2)}) async-start(f32[256,1,128]{2,1,0:T(1,128)} %broadcast_in_dim.17), calls=%async_computation | async-start | bytes 262144 | tf_op jit(solution)/shard_map/all_to_all | solution.py:222

commit v2 on v1

v2 whole, which is shorter than its diff:
```python
import jax
import jax.numpy as jnp
from jax import lax
from jax.experimental import pallas as pl
from jax.experimental.pallas import tpu as pltpu
from jax.sharding import PartitionSpec as P

HEADS = 16
HEAD_DIM = 64
STATE = 256
BLOCK = 256
WIDTH = HEADS * HEAD_DIM
HALF = BLOCK // 2
PAIR = 2 * HEAD_DIM
F32 = jnp.float32
BF16 = jnp.bfloat16
NEG = -1e30
LOG2E = 1.4426950408889634
LEFT = 1500

NN = (((1,), (0,)), ((), ()))
NT = (((1,), (1,)), ((), ()))


def dot(a, b, dims=NN):
    return lax.dot_general(a, b, dims, preferred_element_type=F32)


def split2(v):
    hi = v.astype(BF16)
    return hi, (v - hi.astype(F32)).astype(BF16)


def split3(v):
    hi = v.astype(BF16)
    rest = v - hi.astype(F32)
    mid = rest.astype(BF16)
    return hi, mid, (rest - mid.astype(F32)).astype(BF16)


def softplus(z):
    u = jnp.exp(-jnp.abs(z))
    series = u * (1.0 - u * (0.5 - u * (1.0 / 3.0 - u * 0.25)))
    return jnp.maximum(z, 0.0) + jnp.where(u < 0.01, series, jnp.log(1.0 + u))


def head_rows(count, start=0, width=WIDTH):
    lane = lax.broadcasted_iota(jnp.int32, (count, width), 1) + start
    row = lax.broadcasted_iota(jnp.int32, (count, width), 0)
    hit = lax.shift_right_logical(lane, 6) == (row & (HEADS - 1))
    return (hit & (row < 3 * HEADS)).astype(BF16)


def pieces(v):
    parts = [part.astype(F32) for part in split3(v)]
    rest = jnp.zeros((128 - 3 * HEADS, BLOCK), F32)
    return jnp.concatenate(parts + [rest], axis=0).T.astype(BF16)


def head_sums(v, rows):
    hi, lo = split2(v)
    return dot(rows, hi, NT) + dot(rows, lo, NT)


def triangle(upper):
    r = lax.broadcasted_iota(jnp.int32, (BLOCK, BLOCK), 0)
    c = lax.broadcasted_iota(jnp.int32, (BLOCK, BLOCK), 1)
    return ((r <= c) if upper else (r >= c)).astype(BF16)


def along_tokens(v, tri):
    count = v.shape[0]
    sums = dot(jnp.concatenate(split3(v), axis=0), tri)
    return sums[0:count] + sums[count : 2 * count] + sums[2 * count :]


def columns(row):
    return jnp.broadcast_to(row, (128, BLOCK)).T


def eye():
    r = lax.broadcasted_iota(jnp.int32, (HEADS, HEADS), 0)
    c = lax.broadcasted_iota(jnp.int32, (HEADS, HEADS), 1)
    return r == c


def to_column(row):
    return jnp.sum(jnp.where(eye(), row, 0.0), axis=1, keepdims=True)


def to_row(column):
    return jnp.sum(jnp.where(eye(), column, 0.0), axis=0, keepdims=True)


def head_arrays(raw, bias, lr):
    ell = jnp.exp(to_column(lr))
    z = raw + to_column(bias)
    s = softplus(z)
    return z, s, ell, s * -ell


def edge_gain(first, doc, s, cum):
    edge = jnp.where(first, doc[:, BLOCK - 1 :], doc[:, 0:1])
    arg = jnp.where(first, cum[:, BLOCK - 1 :] - cum, cum)
    gain = jnp.where(first, s, jnp.ones_like(s))
    return edge, jnp.where(doc == edge, jnp.exp(arg) * gain, 0.0)


PARTS = 4
PART = WIDTH // PARTS


def outgoing_kernel(
    doc_hbm, raw_hbm, bias_hbm, lr_hbm, x_hbm, c_hbm, w_hbm, r_hbm,
    send_hbm,
    doc_ref, raw_ref, bias_ref, lr_ref, v_ref, k_ref, send_ref, sems, out_sems,
):
    core = lax.axis_index("ctx")
    first = core == 0
    small = [
        pltpu.make_async_copy(src, dst, sems.at[n])
        for n, (src, dst) in enumerate(
            ((raw_hbm, raw_ref), (bias_hbm, bias_ref), (lr_hbm, lr_ref), (doc_hbm, doc_ref))
        )
    ]
    for copy in small:
        copy.start()

    def fetch_k(src):
        return pltpu.make_async_copy(src.at[0], k_ref, sems.at[4])

    def fetch_v(src, n):
        lanes = slice(n * PART, (n + 1) * PART)
        return pltpu.make_async_copy(src.at[0, :, lanes], v_ref.at[:, lanes], sems.at[5 + n])

    sources = ((w_hbm, x_hbm), (r_hbm, c_hbm))
    for which in range(2):

        @pl.when(core == which)
        def _():
            fetch_k(sources[which][0]).start()
            for n in range(PARTS):
                fetch_v(sources[which][1], n).start()

    tri = triangle(True)
    for copy in small:
        copy.wait()
    doc = doc_ref[...].astype(F32)
    _, s, _, rate = head_arrays(raw_ref[0], bias_ref[...], lr_ref[...])
    edge, f = edge_gain(first, doc, s, along_tokens(rate, tri))
    by_token = pieces(f)
    send_ref[STATE:] = jnp.broadcast_to(edge, (8, WIDTH))
    out = [pltpu.make_async_copy(send_ref.at[STATE:], send_hbm.at[STATE:], out_sems.at[PARTS])]
    out[0].start()
    fetch_k(w_hbm).wait()
    k = k_ref[...].T
    for n in range(PARTS):
        lanes = slice(n * PART, (n + 1) * PART)
        wide = dot(by_token, head_rows(128, n * PART, PART))
        fetch_v(x_hbm, n).wait()
        hi, lo = split2(v_ref[:, lanes].astype(F32) * wide)
        send_ref[0:STATE, lanes] = dot(k, hi) + dot(k, lo)
        copy = pltpu.make_async_copy(
            send_ref.at[0:STATE, lanes], send_hbm.at[0:STATE, lanes], out_sems.at[n]
        )
        copy.start()
        out.append(copy)
    for copy in out:
        copy.wait()


STEP, GAIN, SIG, ELL, COL, ROW = (HEADS * n for n in range(6))
KEPT = ROW + HEADS
W_RATE, W_BIAS, OWN, EDGE = 0, HEADS, 2 * HEADS, 2 * HEADS + 8


def intra_kernel(
    doc_ref, raw_ref, bias_ref, lr_ref, x_ref, c_ref, w_ref, r_ref,
    dx_ref, dp_ref, heads_ref, aux_ref,
    mask_ref, p_ref,
):
    first = lax.axis_index("ctx") == 0
    doc = doc_ref[...].astype(F32)
    z, s, ell, rate = head_arrays(raw_ref[0], bias_ref[...], lr_ref[...])
    sig = 1.0 / (1.0 + jnp.exp(-z))
    both = along_tokens(jnp.concatenate([rate, sig], axis=0), triangle(True))
    cum, cum_sig = both[0:HEADS], both[HEADS:]
    edge, f = edge_gain(first, doc, s, cum)
    heads_ref[STEP:GAIN] = s
    heads_ref[GAIN:SIG] = f
    heads_ref[SIG:ELL] = sig
    heads_ref[ELL:COL] = jnp.broadcast_to(ell, (HEADS, BLOCK))
    doc_col = columns(doc)
    for t in range(2):
        span = slice(t * HALF, (t + 1) * HALF)
        j = lax.broadcasted_iota(jnp.int32, (BLOCK, HALF), 0)
        i = lax.broadcasted_iota(jnp.int32, (BLOCK, HALF), 1) + t * HALF
        ok = (i >= j) & (doc_col == doc[:, span])
        mask_ref[:, span] = jnp.where(ok, 0.0, NEG)
    p_ref[...] = dot(w_ref[0], r_ref[0], NT)
    dp_ref[...] = jnp.zeros((BLOCK, BLOCK), F32)
    rows2 = cum * LOG2E
    cols2 = jnp.concatenate([(cum - jnp.log(s)) * LOG2E, jnp.zeros((128 - HEADS, BLOCK), F32)], axis=0).T
    lane = lax.broadcasted_iota(jnp.int32, (BLOCK, PAIR), 1)
    for pair in range(HEADS // 2):
        lanes = slice(pair * PAIR, (pair + 1) * PAIR)
        xp, cp = x_ref[0, :, lanes], c_ref[0, :, lanes]
        top = bottom = None
        for odd in range(2):
            h = 2 * pair + odd
            ch = jnp.where((lane < HEAD_DIM) != bool(odd), cp, jnp.zeros_like(cp))
            row = rows2[h : h + 1, :]
            col = cols2[:, h : h + 1]

            def tile(js, isl):
                g = dot(xp[js], ch[isl], NT)
                decay = jnp.exp2((row[:, isl] - col[js]) + mask_ref[js, isl])
                m = decay * p_ref[js, isl]
                dp_ref[js, isl] += decay * g
                hi, lo = split2(m)
                return dot(hi, ch[isl]) + dot(lo, ch[isl]), jnp.sum(m * g, axis=0, keepdims=True)

            d0, e0 = tile(slice(0, HALF), slice(0, BLOCK))
            d1, e1 = tile(slice(HALF, BLOCK), slice(HALF, BLOCK))
            heads_ref[ROW + h : ROW + h + 1, 0:HALF] = e0[:, 0:HALF]
            heads_ref[ROW + h : ROW + h + 1, HALF:] = e0[:, HALF:] + e1
            top = d0 if top is None else top + d0
            bottom = d1 if bottom is None else bottom + d1
        dx_ref[0:HALF, lanes] = top
        dx_ref[HALF:, lanes] = bottom
    rows = head_rows(HEADS)
    x = x_ref[0].astype(F32)
    q = head_sums(x * dx_ref[...], rows)
    heads_ref[COL:ROW] = q
    cx = jnp.sum(c_ref[0].astype(F32) * x, axis=0, keepdims=True)
    skip = sum(dot(rows, part, NT) for part in split3(jnp.broadcast_to(cx, (128, WIDTH))))
    da = heads_ref[ROW:] - q
    over = sig / s
    own_rate = jnp.sum(da * cum, axis=1, keepdims=True)
    own_bias = jnp.sum(q * over - ell * (da * cum_sig), axis=1, keepdims=True)
    own = [to_row(own_rate), to_row(own_bias), to_row(skip[:, 0:1])]
    own = jnp.concatenate(own + [jnp.zeros((1, BLOCK - 3 * HEADS), F32)], axis=1)
    w_rate = jnp.where(first, cum[:, BLOCK - 1 :] - cum, cum)
    w_bias = jnp.where(first, over + ell * (cum_sig - cum_sig[:, BLOCK - 1 :]), -ell * cum_sig)
    aux_ref[W_RATE:W_BIAS] = f * w_rate
    aux_ref[W_BIAS:OWN] = f * w_bias
    aux_ref[OWN:EDGE] = jnp.broadcast_to(own, (8, BLOCK))
    aux_ref[EDGE:] = jnp.broadcast_to(edge, (8, BLOCK))


def joined(got_ref, aux_ref):
    return (got_ref[STATE : STATE + 1, 0:1] == aux_ref[EDGE : EDGE + 1, 0:1]).astype(F32)


def sums_kernel(got_ref, aux_ref, x_ref, c_ref, w_ref, r_ref, sums_ref):
    first = lax.axis_index("ctx") == 0
    v = jnp.where(first, x_ref[0], c_ref[0]).astype(F32)
    k = jnp.where(first, w_ref[0], r_ref[0])
    t_hi, t_lo = split2(got_ref[0:STATE])
    z = dot(k, t_hi) + dot(k, t_lo)
    u = head_sums(v * z, head_rows(HEADS)) * joined(got_ref, aux_ref)
    sum_rate = to_row(jnp.sum(u * aux_ref[W_RATE:W_BIAS], axis=1, keepdims=True))
    sum_bias = to_row(jnp.sum(u * aux_ref[W_BIAS:OWN], axis=1, keepdims=True))
    rest = jnp.zeros((1, 128 - 2 * HEADS), F32)
    cross = jnp.concatenate([sum_rate, sum_bias, rest], axis=1)
    sums_ref[...] = aux_ref[OWN : OWN + 1, 0:128] + cross


def grads_kernel(
    got_ref, aux_ref, heads_ref, skip_ref, x_ref, c_ref, w_ref, r_ref, dxi_ref, dp_ref,
    dx_ref, dw_ref, dr_ref, dstep_ref,
):
    first = lax.axis_index("ctx") == 0
    f = heads_ref[GAIN:SIG] * joined(got_ref, aux_ref)
    wide = dot(pieces(f), head_rows(128))
    c = c_ref[0].astype(F32)
    v = jnp.where(first, x_ref[0], c_ref[0]).astype(F32)
    k = jnp.where(first, w_ref[0], r_ref[0])
    t_hi, t_lo = split2(got_ref[0:STATE])
    zs = (dot(k, t_hi) + dot(k, t_lo)) * wide
    hi, lo = split2(v * wide)
    dk = dot(hi, t_hi, NT) + dot(lo, t_hi, NT) + dot(hi, t_lo, NT)
    zero = jnp.zeros_like(dk)
    hi, lo = split2(dp_ref[...])
    dw = dot(hi, r_ref[0]) + dot(lo, r_ref[0])
    hi, lo = split2(dp_ref[...].T)
    dr = dot(hi, w_ref[0]) + dot(lo, w_ref[0])
    dw_ref[0] = (dw + jnp.where(first, dk, zero)).astype(BF16)
    dr_ref[0] = (dr + jnp.where(first, zero, dk)).astype(BF16)
    gains = dot(pieces(jnp.broadcast_to(to_column(skip_ref[...]), (HEADS, BLOCK))), head_rows(128))
    dx = dxi_ref[...] + jnp.where(first, zs, 0.0) + gains * c
    dx_ref[0] = dx.astype(BF16)
    u = head_sums(v * zs, head_rows(HEADS))
    q = heads_ref[COL:ROW] + jnp.where(first, u, 0.0)
    da = heads_ref[ROW:] - q + jnp.where(first, 0.0, u)
    drate = along_tokens(da, triangle(False))
    drate = drate + jnp.where(first, jnp.sum(u, axis=1, keepdims=True), 0.0)
    dstep = (q / heads_ref[STEP:GAIN] - drate * heads_ref[ELL:COL]) * heads_ref[SIG:ELL]
    dstep_ref[0] = dstep


def call(kernel, outs, scratch=(), limit=40 << 10, flops=0, bytes_accessed=0, **specs):
    return pl.pallas_call(
        kernel,
        out_shape=outs,
        scratch_shapes=list(scratch),
        compiler_params=pltpu.CompilerParams(vmem_limit_bytes=limit << 10),
        cost_estimate=pl.CostEstimate(
            flops=flops, bytes_accessed=bytes_accessed, transcendentals=0
        ),
        **specs,
    )


def shape(dims, dtype=F32):
    return jax.ShapeDtypeStruct(dims, dtype)


def mesh_sum(sums, devices):
    both = lax.all_gather(sums, "ctx", axis=0, tiled=True)
    sums = both[0:1] + both[1:2]
    everyone = jnp.broadcast_to(sums, (devices, 128))
    everyone = lax.all_to_all(everyone, "dp", split_axis=0, concat_axis=0, tiled=True)
    return jnp.sum(everyone, axis=0)


def on_device(x, c, w, r, raw, doc, log_rate, step_bias, skip_gain):
    lr, bias, skip = log_rate[None], step_bias[None], skip_gain[None]
    steps = raw.swapaxes(1, 2)
    hbm = pl.BlockSpec(memory_space=pltpu.HBM)
    send = call(
        outgoing_kernel,
        shape((STATE + 8, WIDTH)),
        scratch=(
            pltpu.VMEM((1, BLOCK), jnp.int32),
            pltpu.VMEM((1, HEADS, BLOCK), F32),
            pltpu.VMEM((1, HEADS), F32),
            pltpu.VMEM((1, HEADS), F32),
            pltpu.VMEM((BLOCK, WIDTH), BF16),
            pltpu.VMEM((BLOCK, STATE), BF16),
            pltpu.VMEM((STATE + 8, WIDTH), F32),
            pltpu.SemaphoreType.DMA((5 + PARTS,)),
            pltpu.SemaphoreType.DMA((PARTS + 1,)),
        ),
        flops=300_000_000,
        bytes_accessed=2 << 20,
        in_specs=[hbm] * 8,
        out_specs=hbm,
        limit=(64 << 10) - LEFT,
    )(doc, steps, bias, lr, x, c, w, r)
    got = lax.ppermute(send, "ctx", [(0, 1), (1, 0)])
    dxi, dp, heads, aux = call(
        intra_kernel,
        (shape((BLOCK, WIDTH)), shape((BLOCK, BLOCK)), shape((KEPT, BLOCK)), shape((EDGE + 8, BLOCK))),
        scratch=[pltpu.VMEM((BLOCK, BLOCK), F32)] * 2,
        flops=2_000_000_000,
        bytes_accessed=4 << 20,
    )(doc, steps, bias, lr, x, c, w, r)
    sums = call(
        sums_kernel,
        shape((1, 128)),
        flops=300_000_000,
        bytes_accessed=2 << 20,
    )(got, aux, x, c, w, r)
    total = mesh_sum(sums, lax.axis_size("dp"))
    grad_x, grad_w, grad_r, grad_step = call(
        grads_kernel,
        (
            shape((1, BLOCK, WIDTH), BF16),
            shape((1, BLOCK, STATE), BF16),
            shape((1, BLOCK, STATE), BF16),
            shape((1, HEADS, BLOCK)),
        ),
        flops=1_000_000_000,
        bytes_accessed=5 << 20,
    )(got, aux, heads, skip, x, c, w, r, dxi, dp)
    return (
        grad_x, grad_w, grad_r, grad_step.swapaxes(1, 2),
        total[0:HEADS], total[HEADS : 2 * HEADS], total[2 * HEADS : 3 * HEADS],
    )


def solution(mesh):
    split = P("dp", "ctx", None)
    return jax.shard_map(
        on_device,
        mesh=mesh,
        in_specs=(split, split, split, split, split, P("dp", "ctx"), P(), P(), P()),
        out_specs=(split, split, split, split, P(), P(), P()),
        check_vma=False,
    )
```

time: 57.4 us -> 50.2 us (0.87)
  local copies, waits for them, and re-layouts: 8.74 us -> 2.58 us
  waiting for transfers between devices: 11.4 us -> 8.29 us
  Pallas kernels: 7.92 us -> 10.7 us
  blocking collectives: 2.45 us -> 1.76 us
    unnamed x24 -> x22, local copies, waits for them, and re-layouts: 7.42 us -> 1.26 us
    all_to_all x1, waiting for transfers between devices: 11.4 us -> 8.29 us  [mesh_sum(): lax.all_to_all(everyone, 'dp', split_axis=0, concat_axis=0, tiled=True)]
    pallas_call x3 -> x4, Pallas kernels: 7.92 us -> 10.7 us  [the longest x1 3.52 us: on_device(): call(outgoing_kernel, shape((STATE + 8, WIDTH)), scratch=(pltpu.VMEM((1,...]
    psum x1 -> x0, blocking collectives: 2.45 us -> none  [mesh_sum(): sums = lax.psum(sums, 'ctx')]
    all_gather x0 -> x1, blocking collectives: none -> 1.76 us  [mesh_sum(): both = lax.all_gather(sums, 'ctx', axis=0, tiled=True)]
  transfers between devices with their start and end apart: 2 -> 2, of which waited for: 1 -> 1; matrix products, arithmetic and copies ran while one was open for 1% -> 0% of each run, Pallas kernels for 5% -> 12%
where the time goes in v2:
time: 50.2 us; the launch traced here: 50 us
  starting transfers between devices  25.8 us (51%)
  Pallas kernels  10.7 us (21%)
  waiting for transfers between devices  8.29 us (17%)
  local copies, waits for them, and re-layouts  2.58 us (5%)
  blocking collectives  1.76 us (4%)
  between operations  0.84 us (2%)
    all_to_all x1, starting transfers between devices, mesh_sum(): lax.all_to_all(everyone, 'dp', split_axis=0, concat_axis=0, tiled=True)  17 us
    ppermute x1, starting transfers between devices, on_device(): got = lax.ppermute(send, 'ctx', [(0, 1), (1, 0)])  8.79 us
    all_to_all x1, waiting for transfers between devices, mesh_sum(): lax.all_to_all(everyone, 'dp', split_axis=0, concat_axis=0, tiled=True)  8.29 us
    pallas_call x1, Pallas kernels, on_device(): call(outgoing_kernel, shape((STATE + 8, WIDTH)), scratch=(pltpu.VMEM((1,...  3.52 us
    pallas_call x1, Pallas kernels, on_device(): call(intra_kernel, (shape((BLOCK, WIDTH)), shape((BLOCK, BLOCK)), shape((...  3.39 us
    pallas_call x1, Pallas kernels, on_device(): call(grads_kernel, (shape((1, BLOCK, WIDTH), BF16), shape((1, BLOCK, STAT...  2.52 us
    all_gather x1, blocking collectives, mesh_sum(): both = lax.all_gather(sums, 'ctx', axis=0, tiled=True)  1.76 us
    unnamed x22, local copies, waits for them, and re-layouts  1.26 us
  transfers between devices with their start and end apart: 2, of which 1 were waited for; matrix products, arithmetic and copies ran while one was open for 0% of the time, Pallas kernels for 12%

profile of v2, /device:TPU:1, one launch (start us, length us, event | category | flops | bytes accessed | tf_op | source)
XLA Modules:
  0.0 50.0 jit_solution(4663473281184481559)
XLA Ops:
  0.6 0.0 copy-start
  0.6 0.0 copy-start.1
  0.7 0.0 copy-start.2
  0.7 0.0 copy-start.3
  0.7 0.0 copy-start.6
  0.7 0.0 copy-start.7
  0.7 0.0 copy-start.9
  0.7 0.0 copy-start.10
  0.7 3.5 %shard_map.144 = f32[264,1024]{1,0:T(8,128)} custom-call(s32[1,256]{1,0:T(1,128)} %doc_ref.1, f32[1,16,256]{2,1,0:T(8,128)} %bitcast.9, f32[1,16]{1,0:T(1,128)} %bitcast.12, f32[1,16]{1,0:T(1,128)} %bitcast.14, bf16[1,256,1024]{2,1,0:T(8,128)(2,1)} %x_ref.5, bf16[1,256,1024]{2,1,0:T(8,128)(2,1)} %c_ref.5, bf16[1,256,256]{2,1,0:T(8,128)(2,1)} %w_ref.5, ...), custom_call_target="tpu_custom_call" | custom-call | flops 300000000 | bytes 2097152 | tf_op jit(solution)/shard_map/pallas_call | solution.py:331
  4.2 8.8 %collective-permute-start = (f32[264,1024]{1,0:T(8,128)}, f32[264,1024]{1,0:T(8,128)S(1)}, u32[]{:S(2)}, u32[]{:S(2)}) collective-permute-start(f32[264,1024]{1,0:T(8,128)} %shard_map.144), channel_id=1, source_target_pairs={{0,1},{1,0},{2,3},{3,2},{4,5},{5,4},{6,7},{7,6},{8,9},{9,8},{10,11... | collective-permute-start | bytes 3244040 | tf_op jit(solution)/shard_map/ppermute | solution.py:351
  13.0 0.0 copy-done
  13.1 0.0 copy-done.1
  13.1 0.0 copy-done.2
  13.1 0.0 copy-done.3
  13.1 0.0 copy-done.6
  13.1 0.0 copy-done.7
  13.1 0.0 copy-done.9
  13.1 0.0 copy-done.10
  13.1 3.4 %shard_map.145 = (f32[256,1024]{1,0:T(8,128)S(1)}, f32[256,256]{1,0:T(8,128)S(1)}, f32[96,256]{1,0:T(8,128)S(1)}, f32[48,256]{1,0:T(8,128)S(1)}) custom-call(s32[1,256]{1,0:T(1,128)S(1)} %copy-done.7, f32[1,16,256]{2,1,0:T(8,128)S(1)} %bitcast.10, f32[1,16]{1,0:T(1,128)S(1)} %bitcast.13, f32[1,16]{1,0:T(1,128)S(1)} %bitcast.15, ...), custom_call_target="tpu_custom_call" | custom-call | flops 2000000000 | bytes 4194304 | tf_op jit(solution)/shard_map/pallas_call | solution.py:352
  16.5 0.0 copy-start.4
  16.5 0.0 collective-permute-done.got_ref
  16.5 0.0 copy-start.8
  16.5 1.3 %shard_map.147 = f32[1,128]{1,0:T(1,128)S(1)} custom-call(f32[264,1024]{1,0:T(8,128)S(1)} %collective-permute-done.got_ref, f32[48,256]{1,0:T(8,128)S(1)} %get-tuple-element.15.aux_ref, bf16[1,256,1024]{2,1,0:T(8,128)(2,1)S(1)} %copy-done, bf16[1,256,1024]{2,1,0:T(8,128)(2,1)S(1)} %copy-done.1, bf16[1,256,256]{2,1,0:T(8,128)(2,1)S(1)} %copy-done.2, ...), custom_call_target="tpu_custom_call" | custom-call | flops 300000000 | bytes 2097152 | tf_op jit(solution)/shard_map/pallas_call | solution.py:359
  17.8 0.0 copy-done.4
  17.8 1.8 %all-gather = f32[2,1,128]{2,1,0:T(1,128)S(1)} all-gather(f32[1,1,128]{2,1,0:T(1,128)S(1)} %bitcast.16), channel_id=1, replica_groups=mesh['dp'=256,'ctx'=2] {'ctx'}, dimensions={0}, use_global_device_ids=true | all-gather | bytes 1536 | tf_op jit(solution)/shard_map/all_gather | solution.py:320
  19.6 0.7 %broadcast_in_dim.17 = f32[256,1,128]{2,1,0:T(1,128)} broadcast(f32[128]{0:T(128)S(1)} %fusion), dimensions={2} | broadcast | bytes 131584 | tf_op jit(solution)/shard_map/broadcast_in_dim | solution.py:322
  20.3 17.0 %all-to-all-start = ((f32[256,1,128]{2,1,0:T(1,128)}), f32[256,1,128]{2,1,0:T(1,128)S(1)}, u32[]{:S(2)}, u32[]{:S(2)}) async-start(f32[256,1,128]{2,1,0:T(1,128)} %broadcast_in_dim.17), calls=%async_computation | async-start | bytes 262144 | tf_op jit(solution)/shard_map/all_to_all | solution.py:323
  37.3 0.0 copy-done.8
  37.3 1.2 %copy-done.5 = f32[256,1024]{1,0:T(8,128)S(1)} copy-done((f32[256,1024]{1,0:T(8,128)S(1)}, f32[256,1024]{1,0:T(8,128)}, u32[]{:S(2)}) %copy-start.5) | copy-done | bytes 1048600
  38.5 2.5 %shard_map.146 = (bf16[1,256,1024]{2,1,0:T(8,128)(2,1)}, bf16[1,256,256]{2,1,0:T(8,128)(2,1)}, bf16[1,256,256]{2,1,0:T(8,128)(2,1)}, f32[1,16,256]{2,1,0:T(8,128)}) custom-call(f32[264,1024]{1,0:T(8,128)S(1)} %collective-permute-done.got_ref, f32[48,256]{1,0:T(8,128)S(1)} %get-tuple-element.15.aux_ref, f32[96,256]{1,0:T(8,128)S(1)} %get-tuple-element.16.heads_ref, ...), custom_call_target="tpu_custom_call" | custom-call | flops 1000000000 | bytes 5242880 | tf_op jit(solution)/shard_map/pallas_call | solution.py:366
  41.1 8.3 %all-to-all-done = f32[256,1,128]{2,1,0:T(1,128)S(1)} async-done(((f32[256,1,128]{2,1,0:T(1,128)}), f32[256,1,128]{2,1,0:T(1,128)S(1)}, u32[]{:S(2)}, u32[]{:S(2)}) %all-to-all-start) | async-done | bytes 131104 | tf_op jit(solution)/shard_map/all_to_all | solution.py:323
  49.4 0.6 %fusion.1 = (f32[16]{0:T(128)}, f32[16]{0:T(128)}, f32[16]{0:T(128)}) fusion(f32[128]{0:T(128)S(1)} %reduce_sum.9), kind=kLoop, calls=%fused_computation.2 | loop fusion | bytes 384 | tf_op jit(solution)/shard_map/slice | solution.py:379
  (3 shorter events, 0.1 us)
Async XLA Ops:
  0.6 12.4 %copy-start = (bf16[1,256,1024]{2,1,0:T(8,128)(2,1)S(1)}, bf16[1,256,1024]{2,1,0:T(8,128)(2,1)}, u32[]{:S(2)}) copy-start(bf16[1,256,1024]{2,1,0:T(8,128)(2,1)} %x_ref.5) | copy-start | bytes 1572868
  0.6 12.4 %copy-start.1 = (bf16[1,256,1024]{2,1,0:T(8,128)(2,1)S(1)}, bf16[1,256,1024]{2,1,0:T(8,128)(2,1)}, u32[]{:S(2)}) copy-start(bf16[1,256,1024]{2,1,0:T(8,128)(2,1)} %c_ref.5) | copy-start | bytes 1572868
  0.7 12.4 %copy-start.2 = (bf16[1,256,256]{2,1,0:T(8,128)(2,1)S(1)}, bf16[1,256,256]{2,1,0:T(8,128)(2,1)}, u32[]{:S(2)}) copy-start(bf16[1,256,256]{2,1,0:T(8,128)(2,1)} %w_ref.5) | copy-start | bytes 393220
  0.7 12.4 %copy-start.3 = (bf16[1,256,256]{2,1,0:T(8,128)(2,1)S(1)}, bf16[1,256,256]{2,1,0:T(8,128)(2,1)}, u32[]{:S(2)}) copy-start(bf16[1,256,256]{2,1,0:T(8,128)(2,1)} %r_ref.5) | copy-start | bytes 393220
  0.7 12.4 %copy-start.6 = (f32[1,256,16]{1,2,0:T(8,128)S(1)}, f32[1,256,16]{1,2,0:T(8,128)}, u32[]{:S(2)}) copy-start(f32[1,256,16]{1,2,0:T(8,128)} %param.13) | copy-start | bytes 49156
  0.7 12.4 %copy-start.7 = (s32[1,256]{1,0:T(1,128)S(1)}, s32[1,256]{1,0:T(1,128)}, u32[]{:S(2)}) copy-start(s32[1,256]{1,0:T(1,128)} %doc_ref.1) | copy-start | bytes 3076
  0.7 12.4 %copy-start.9 = (f32[16]{0:T(128)S(1)}, f32[16]{0:T(128)}, u32[]{:S(2)}) copy-start(f32[16]{0:T(128)} %param.16) | copy-start | bytes 196
  0.7 12.4 %copy-start.10 = (f32[16]{0:T(128)S(1)}, f32[16]{0:T(128)}, u32[]{:S(2)}) copy-start(f32[16]{0:T(128)} %param.15) | copy-start | bytes 196
  4.2 12.3 %collective-permute-start = (f32[264,1024]{1,0:T(8,128)}, f32[264,1024]{1,0:T(8,128)S(1)}, u32[]{:S(2)}, u32[]{:S(2)}) collective-permute-start(f32[264,1024]{1,0:T(8,128)} %shard_map.144), channel_id=1, source_target_pairs={{0,1},{1,0},{2,3},{3,2},{4,5},{5,4},{6,7},{7,6},{8,9},{9,8},{10,11... | collective-permute-start | bytes 3244040 | tf_op jit(solution)/shard_map/ppermute | solution.py:351
  16.5 1.3 %copy-start.4 = (f32[256,1024]{1,0:T(8,128)}, f32[256,1024]{1,0:T(8,128)S(1)}, u32[]{:S(2)}) copy-start(f32[256,1024]{1,0:T(8,128)S(1)} %get-tuple-element.17.dxi_ref) | copy-start | bytes 3145732
  16.5 20.8 %copy-start.8 = (f32[16]{0:T(128)S(1)}, f32[16]{0:T(128)}, u32[]{:S(2)}) copy-start(f32[16]{0:T(128)} %param.17) | copy-start | bytes 196
  20.3 29.0 %all-to-all-start = ((f32[256,1,128]{2,1,0:T(1,128)}), f32[256,1,128]{2,1,0:T(1,128)S(1)}, u32[]{:S(2)}, u32[]{:S(2)}) async-start(f32[256,1,128]{2,1,0:T(1,128)} %broadcast_in_dim.17), calls=%async_computation | async-start | bytes 262144 | tf_op jit(solution)/shard_map/all_to_all | solution.py:323
  37.3 1.2 %copy-start.5 = (f32[256,1024]{1,0:T(8,128)S(1)}, f32[256,1024]{1,0:T(8,128)}, u32[]{:S(2)}) copy-start(f32[256,1024]{1,0:T(8,128)} %copy-done.4) | copy-start | bytes 3145732

commit v3 on v2

--- a/solution.py
+++ b/solution.py
@@ -16,7 +16,6 @@
 BF16 = jnp.bfloat16
 NEG = -1e30
 LOG2E = 1.4426950408889634
-LEFT = 1500
 
 NN = (((1,), (0,)), ((), ()))
 NT = (((1,), (1,)), ((), ()))
@@ -108,17 +107,25 @@
 
 PARTS = 4
 PART = WIDTH // PARTS
+STEP, GAIN, SIG, ELL, CUM, CUM_SIG, EDGE = (HEADS * n for n in range(7))
+KEPT = EDGE + 8
+COL, ROW = 0, HEADS
+W_RATE, W_BIAS, OWN = 0, HEADS, 2 * HEADS
 
 
 def outgoing_kernel(
     doc_hbm, raw_hbm, bias_hbm, lr_hbm, x_hbm, c_hbm, w_hbm, r_hbm,
-    send_hbm,
-    doc_ref, raw_ref, bias_ref, lr_ref, v_ref, k_ref, send_ref, sems, out_sems,
+    send_ref, heads_ref, x_ref, c_ref, w_ref, r_ref,
+    doc_ref, raw_ref, bias_ref, lr_ref, sems,
 ):
     core = lax.axis_index("ctx")
     first = core == 0
+
+    def fetch(src, dst, n):
+        return pltpu.make_async_copy(src, dst, sems.at[n])
+
     small = [
-        pltpu.make_async_copy(src, dst, sems.at[n])
+        fetch(src, dst, n)
         for n, (src, dst) in enumerate(
             ((raw_hbm, raw_ref), (bias_hbm, bias_ref), (lr_hbm, lr_ref), (doc_hbm, doc_ref))
         )
@@ -126,70 +133,74 @@
     for copy in small:
         copy.start()
 
-    def fetch_k(src):
-        return pltpu.make_async_copy(src.at[0], k_ref, sems.at[4])
-
-    def fetch_v(src, n):
-        lanes = slice(n * PART, (n + 1) * PART)
-        return pltpu.make_async_copy(src.at[0, :, lanes], v_ref.at[:, lanes], sems.at[5 + n])
-
-    sources = ((w_hbm, x_hbm), (r_hbm, c_hbm))
-    for which in range(2):
-
-        @pl.when(core == which)
-        def _():
-            fetch_k(sources[which][0]).start()
-            for n in range(PARTS):
-                fetch_v(sources[which][1], n).start()
+    def rows_of(src, dst, base):
+        part = BLOCK // PARTS
+        spans = [pl.ds(n * part, part) for n in range(PARTS)]
+        return [fetch(src.at[:, span], dst.at[:, span], base + n) for n, span in enumerate(spans)]
+
+    fetch_w, fetch_r = fetch(w_hbm, w_ref, 4), fetch(r_hbm, r_ref, 5)
+    fetch_x, fetch_c = rows_of(x_hbm, x_ref, 6), rows_of(c_hbm, c_ref, 6 + PARTS)
+
+    @pl.when(first)
+    def _():
+        for copy in [fetch_w] + fetch_x + [fetch_r] + fetch_c:
+            copy.start()
+
+    @pl.when(core == 1)
+    def _():
+        for copy in [fetch_r] + fetch_c + [fetch_w] + fetch_x:
+            copy.start()
 
     tri = triangle(True)
     for copy in small:
         copy.wait()
     doc = doc_ref[...].astype(F32)
-    _, s, _, rate = head_arrays(raw_ref[0], bias_ref[...], lr_ref[...])
-    edge, f = edge_gain(first, doc, s, along_tokens(rate, tri))
+    z, s, ell, rate = head_arrays(raw_ref[0], bias_ref[...], lr_ref[...])
+    sig = 1.0 / (1.0 + jnp.exp(-z))
+    both = along_tokens(jnp.concatenate([rate, sig], axis=0), tri)
+    edge, f = edge_gain(first, doc, s, both[0:HEADS])
+    heads_ref[STEP:GAIN] = s
+    heads_ref[GAIN:SIG] = f
+    heads_ref[SIG:ELL] = sig
+    heads_ref[ELL:CUM] = jnp.broadcast_to(ell, (HEADS, BLOCK))
+    heads_ref[CUM:EDGE] = both
+    heads_ref[EDGE:] = jnp.broadcast_to(edge, (8, BLOCK))
+    send_ref[STATE:] = jnp.broadcast_to(edge, (8, WIDTH))
     by_token = pieces(f)
-    send_ref[STATE:] = jnp.broadcast_to(edge, (8, WIDTH))
-    out = [pltpu.make_async_copy(send_ref.at[STATE:], send_hbm.at[STATE:], out_sems.at[PARTS])]
-    out[0].start()
-    fetch_k(w_hbm).wait()
-    k = k_ref[...].T
-    for n in range(PARTS):
-        lanes = slice(n * PART, (n + 1) * PART)
-        wide = dot(by_token, head_rows(128, n * PART, PART))
-        fetch_v(x_hbm, n).wait()
-        hi, lo = split2(v_ref[:, lanes].astype(F32) * wide)
-        send_ref[0:STATE, lanes] = dot(k, hi) + dot(k, lo)
-        copy = pltpu.make_async_copy(
-            send_ref.at[0:STATE, lanes], send_hbm.at[0:STATE, lanes], out_sems.at[n]
-        )
-        copy.start()
-        out.append(copy)
-    for copy in out:
-        copy.wait()
-
-
-STEP, GAIN, SIG, ELL, COL, ROW = (HEADS * n for n in range(6))
-KEPT = ROW + HEADS
-W_RATE, W_BIAS, OWN, EDGE = 0, HEADS, 2 * HEADS, 2 * HEADS + 8
+
+    def make_state(fetch_k, k_ref, fetch_v, v_ref):
+        fetch_k.wait()
+        k = k_ref[0].T
+        for copy in fetch_v:
+            copy.wait()
+        for n in range(PARTS):
+            lanes = slice(n * PART, (n + 1) * PART)
+            wide = dot(by_token, head_rows(128, n * PART, PART))
+            hi, lo = split2(v_ref[0, :, lanes].astype(F32) * wide)
+            send_ref[0:STATE, lanes] = dot(k, hi) + dot(k, lo)
+
+    @pl.when(first)
+    def _():
+        make_state(fetch_w, w_ref, fetch_x, x_ref)
+        for copy in [fetch_r] + fetch_c:
+            copy.wait()
+
+    @pl.when(core == 1)
+    def _():
+        make_state(fetch_r, r_ref, fetch_c, c_ref)
+        for copy in [fetch_w] + fetch_x:
+            copy.wait()
 
 
 def intra_kernel(
-    doc_ref, raw_ref, bias_ref, lr_ref, x_ref, c_ref, w_ref, r_ref,
-    dx_ref, dp_ref, heads_ref, aux_ref,
+    doc_ref, heads_ref, x_ref, c_ref, w_ref, r_ref,
+    dx_ref, dp_ref, stat_ref, aux_ref,
     mask_ref, p_ref,
 ):
     first = lax.axis_index("ctx") == 0
     doc = doc_ref[...].astype(F32)
-    z, s, ell, rate = head_arrays(raw_ref[0], bias_ref[...], lr_ref[...])
-    sig = 1.0 / (1.0 + jnp.exp(-z))
-    both = along_tokens(jnp.concatenate([rate, sig], axis=0), triangle(True))
-    cum, cum_sig = both[0:HEADS], both[HEADS:]
-    edge, f = edge_gain(first, doc, s, cum)
-    heads_ref[STEP:GAIN] = s
-    heads_ref[GAIN:SIG] = f
-    heads_ref[SIG:ELL] = sig
-    heads_ref[ELL:COL] = jnp.broadcast_to(ell, (HEADS, BLOCK))
+    s, f, sig = heads_ref[STEP:GAIN], heads_ref[GAIN:SIG], heads_ref[SIG:ELL]
+    ell, cum, cum_sig = heads_ref[ELL:CUM], heads_ref[CUM:CUM_SIG], heads_ref[CUM_SIG:EDGE]
     doc_col = columns(doc)
     for t in range(2):
         span = slice(t * HALF, (t + 1) * HALF)
@@ -222,8 +233,8 @@
 
             d0, e0 = tile(slice(0, HALF), slice(0, BLOCK))
             d1, e1 = tile(slice(HALF, BLOCK), slice(HALF, BLOCK))
-            heads_ref[ROW + h : ROW + h + 1, 0:HALF] = e0[:, 0:HALF]
-            heads_ref[ROW + h : ROW + h + 1, HALF:] = e0[:, HALF:] + e1
+            stat_ref[ROW + h : ROW + h + 1, 0:HALF] = e0[:, 0:HALF]
+            stat_ref[ROW + h : ROW + h + 1, HALF:] = e0[:, HALF:] + e1
             top = d0 if top is None else top + d0
             bottom = d1 if bottom is None else bottom + d1
         dx_ref[0:HALF, lanes] = top
@@ -231,10 +242,10 @@
     rows = head_rows(HEADS)
     x = x_ref[0].astype(F32)
     q = head_sums(x * dx_ref[...], rows)
-    heads_ref[COL:ROW] = q
+    stat_ref[COL:ROW] = q
     cx = jnp.sum(c_ref[0].astype(F32) * x, axis=0, keepdims=True)
     skip = sum(dot(rows, part, NT) for part in split3(jnp.broadcast_to(cx, (128, WIDTH))))
-    da = heads_ref[ROW:] - q
+    da = stat_ref[ROW:] - q
     over = sig / s
     own_rate = jnp.sum(da * cum, axis=1, keepdims=True)
     own_bias = jnp.sum(q * over - ell * (da * cum_sig), axis=1, keepdims=True)
@@ -244,21 +255,20 @@
     w_bias = jnp.where(first, over + ell * (cum_sig - cum_sig[:, BLOCK - 1 :]), -ell * cum_sig)
     aux_ref[W_RATE:W_BIAS] = f * w_rate
     aux_ref[W_BIAS:OWN] = f * w_bias
-    aux_ref[OWN:EDGE] = jnp.broadcast_to(own, (8, BLOCK))
-    aux_ref[EDGE:] = jnp.broadcast_to(edge, (8, BLOCK))
-
-
-def joined(got_ref, aux_ref):
-    return (got_ref[STATE : STATE + 1, 0:1] == aux_ref[EDGE : EDGE + 1, 0:1]).astype(F32)
-
-
-def sums_kernel(got_ref, aux_ref, x_ref, c_ref, w_ref, r_ref, sums_ref):
+    aux_ref[OWN:] = jnp.broadcast_to(own, (8, BLOCK))
+
+
+def joined(got_ref, heads_ref):
+    return (got_ref[STATE : STATE + 1, 0:1] == heads_ref[EDGE : EDGE + 1, 0:1]).astype(F32)
+
+
+def sums_kernel(got_ref, heads_ref, aux_ref, x_ref, c_ref, w_ref, r_ref, sums_ref):
     first = lax.axis_index("ctx") == 0
     v = jnp.where(first, x_ref[0], c_ref[0]).astype(F32)
     k = jnp.where(first, w_ref[0], r_ref[0])
     t_hi, t_lo = split2(got_ref[0:STATE])
     z = dot(k, t_hi) + dot(k, t_lo)
-    u = head_sums(v * z, head_rows(HEADS)) * joined(got_ref, aux_ref)
+    u = head_sums(v * z, head_rows(HEADS)) * joined(got_ref, heads_ref)
     sum_rate = to_row(jnp.sum(u * aux_ref[W_RATE:W_BIAS], axis=1, keepdims=True))
     sum_bias = to_row(jnp.sum(u * aux_ref[W_BIAS:OWN], axis=1, keepdims=True))
     rest = jnp.zeros((1, 128 - 2 * HEADS), F32)
@@ -267,11 +277,11 @@
 
 
 def grads_kernel(
-    got_ref, aux_ref, heads_ref, skip_ref, x_ref, c_ref, w_ref, r_ref, dxi_ref, dp_ref,
+    got_ref, heads_ref, stat_ref, skip_ref, x_ref, c_ref, w_ref, r_ref, dxi_ref, dp_ref,
     dx_ref, dw_ref, dr_ref, dstep_ref,
 ):
     first = lax.axis_index("ctx") == 0
-    f = heads_ref[GAIN:SIG] * joined(got_ref, aux_ref)
+    f = heads_ref[GAIN:SIG] * joined(got_ref, heads_ref)
     wide = dot(pieces(f), head_rows(128))
     c = c_ref[0].astype(F32)
     v = jnp.where(first, x_ref[0], c_ref[0]).astype(F32)
@@ -291,11 +301,11 @@
     dx = dxi_ref[...] + jnp.where(first, zs, 0.0) + gains * c
     dx_ref[0] = dx.astype(BF16)
     u = head_sums(v * zs, head_rows(HEADS))
-    q = heads_ref[COL:ROW] + jnp.where(first, u, 0.0)
-    da = heads_ref[ROW:] - q + jnp.where(first, 0.0, u)
+    q = stat_ref[COL:ROW] + jnp.where(first, u, 0.0)
+    da = stat_ref[ROW:] - q + jnp.where(first, 0.0, u)
     drate = along_tokens(da, triangle(False))
     drate = drate + jnp.where(first, jnp.sum(u, axis=1, keepdims=True), 0.0)
-    dstep = (q / heads_ref[STEP:GAIN] - drate * heads_ref[ELL:COL]) * heads_ref[SIG:ELL]
+    dstep = (q / heads_ref[STEP:GAIN] - drate * heads_ref[ELL:CUM]) * heads_ref[SIG:ELL]
     dstep_ref[0] = dstep
 
 
@@ -327,41 +337,36 @@
 def on_device(x, c, w, r, raw, doc, log_rate, step_bias, skip_gain):
     lr, bias, skip = log_rate[None], step_bias[None], skip_gain[None]
     steps = raw.swapaxes(1, 2)
-    hbm = pl.BlockSpec(memory_space=pltpu.HBM)
-    send = call(
+    square, rows = shape((1, BLOCK, STATE), BF16), shape((1, BLOCK, WIDTH), BF16)
+    inputs = [pltpu.with_memory_space_constraint(a, pltpu.HBM) for a in (doc, steps, bias, lr, x, c, w, r)]
+    send, heads, x, c, w, r = call(
         outgoing_kernel,
-        shape((STATE + 8, WIDTH)),
+        (shape((STATE + 8, WIDTH)), shape((KEPT, BLOCK)), rows, rows, square, square),
         scratch=(
             pltpu.VMEM((1, BLOCK), jnp.int32),
             pltpu.VMEM((1, HEADS, BLOCK), F32),
             pltpu.VMEM((1, HEADS), F32),
             pltpu.VMEM((1, HEADS), F32),
-            pltpu.VMEM((BLOCK, WIDTH), BF16),
-            pltpu.VMEM((BLOCK, STATE), BF16),
-            pltpu.VMEM((STATE + 8, WIDTH), F32),
-            pltpu.SemaphoreType.DMA((5 + PARTS,)),
-            pltpu.SemaphoreType.DMA((PARTS + 1,)),
+            pltpu.SemaphoreType.DMA((6 + 2 * PARTS,)),
         ),
         flops=300_000_000,
         bytes_accessed=2 << 20,
-        in_specs=[hbm] * 8,
-        out_specs=hbm,
-        limit=(64 << 10) - LEFT,
-    )(doc, steps, bias, lr, x, c, w, r)
+        in_specs=[pl.BlockSpec(memory_space=pltpu.HBM)] * 8,
+    )(*inputs)
     got = lax.ppermute(send, "ctx", [(0, 1), (1, 0)])
-    dxi, dp, heads, aux = call(
+    dxi, dp, stat, aux = call(
         intra_kernel,
-        (shape((BLOCK, WIDTH)), shape((BLOCK, BLOCK)), shape((KEPT, BLOCK)), shape((EDGE + 8, BLOCK))),
+        (shape((BLOCK, WIDTH)), shape((BLOCK, BLOCK)), shape((2 * HEADS, BLOCK)), shape((OWN + 8, BLOCK))),
         scratch=[pltpu.VMEM((BLOCK, BLOCK), F32)] * 2,
         flops=2_000_000_000,
         bytes_accessed=4 << 20,
-    )(doc, steps, bias, lr, x, c, w, r)
+    )(doc, heads, x, c, w, r)
     sums = call(
         sums_kernel,
         shape((1, 128)),
         flops=300_000_000,
         bytes_accessed=2 << 20,
-    )(got, aux, x, c, w, r)
+    )(got, heads, aux, x, c, w, r)
     total = mesh_sum(sums, lax.axis_size("dp"))
     grad_x, grad_w, grad_r, grad_step = call(
         grads_kernel,
@@ -373,7 +378,7 @@
         ),
         flops=1_000_000_000,
         bytes_accessed=5 << 20,
-    )(got, aux, heads, skip, x, c, w, r, dxi, dp)
+    )(got, heads, stat, skip, x, c, w, r, dxi, dp)
     return (
         grad_x, grad_w, grad_r, grad_step.swapaxes(1, 2),
         total[0:HEADS], total[HEADS : 2 * HEADS], total[2 * HEADS : 3 * HEADS],

time: 50.2 us -> 50.3 us (level)
  Pallas kernels: 10.7 us -> 9.27 us
  starting transfers between devices: 25.8 us -> 26.9 us
  waiting for transfers between devices: 8.29 us -> 7.3 us
  other arithmetic: 0.05 us -> 0.95 us
    pallas_call x1, Pallas kernels: 3.52 us -> 2.22 us  [on_device(): call(outgoing_kernel, (shape((STATE + 8, WIDTH)), shape((KEPT, BLOCK)), r...]
    all_to_all x1, starting transfers between devices: 17 us -> 18.1 us  [mesh_sum(): lax.all_to_all(everyone, 'dp', split_axis=0, concat_axis=0, tiled=True)]
    all_to_all x1, waiting for transfers between devices: 8.29 us -> 7.3 us  [mesh_sum(): lax.all_to_all(everyone, 'dp', split_axis=0, concat_axis=0, tiled=True)]
    reduce_sum x1, other arithmetic: 0.05 us -> 0.95 us  [mesh_sum(): return jnp.sum(everyone, axis=0)]
    unnamed x22 -> x12, local copies, waits for them, and re-layouts: 1.26 us -> 1.72 us
where the time goes in v3:
time: 50.3 us; the launch traced here: 49.9 us
  starting transfers between devices  26.9 us (53%)
  Pallas kernels  9.27 us (18%)
  waiting for transfers between devices  7.3 us (15%)
  local copies, waits for them, and re-layouts  3.06 us (6%)
  blocking collectives  1.76 us (3%)
  other arithmetic  0.95 us (2%)
  between operations  0.71 us (1%)
    all_to_all x1, starting transfers between devices, mesh_sum(): lax.all_to_all(everyone, 'dp', split_axis=0, concat_axis=0, tiled=True)  18.1 us
    ppermute x1, starting transfers between devices, on_device(): got = lax.ppermute(send, 'ctx', [(0, 1), (1, 0)])  8.79 us
    all_to_all x1, waiting for transfers between devices, mesh_sum(): lax.all_to_all(everyone, 'dp', split_axis=0, concat_axis=0, tiled=True)  7.3 us
    pallas_call x1, Pallas kernels, on_device(): call(intra_kernel, (shape((BLOCK, WIDTH)), shape((BLOCK, BLOCK)), shape((...  3.27 us
    pallas_call x1, Pallas kernels, on_device(): call(grads_kernel, (shape((1, BLOCK, WIDTH), BF16), shape((1, BLOCK, STAT...  2.52 us
    pallas_call x1, Pallas kernels, on_device(): call(outgoing_kernel, (shape((STATE + 8, WIDTH)), shape((KEPT, BLOCK)), r...  2.22 us
    all_gather x1, blocking collectives, mesh_sum(): both = lax.all_gather(sums, 'ctx', axis=0, tiled=True)  1.76 us
    unnamed x12, local copies, waits for them, and re-layouts  1.72 us
  transfers between devices with their start and end apart: 2, of which 1 were waited for; matrix products, arithmetic and copies ran while one was open for 0% of the time, Pallas kernels for 12%

profile of v3, /device:TPU:1, one launch (start us, length us, event | category | flops | bytes accessed | tf_op | source)
XLA Modules:
  0.0 49.9 jit_solution(7290110497026891383)
XLA Ops:
  0.6 0.0 copy-start.4
  0.6 2.2 %shard_map.144 = (f32[264,1024]{1,0:T(8,128)S(1)}, f32[104,256]{1,0:T(8,128)S(1)}, bf16[1,256,1024]{2,1,0:T(8,128)(2,1)S(1)}, bf16[1,256,1024]{2,1,0:T(8,128)(2,...) custom-call(s32[1,256]{1,0:T(1,128)} %doc_ref.1, f32[1,16,256]{2,1,0:T(8,128)} %bitcast.11, ...), custom_call_target="tpu_custom_call" | custom-call | flops 300000000 | bytes 2097152 | tf_op jit(solution)/shard_map/pallas_call | solution.py:342
  2.9 8.8 %collective-permute-start = (f32[264,1024]{1,0:T(8,128)S(1)}, f32[264,1024]{1,0:T(8,128)S(1)}, u32[]{:S(2)}, u32[]{:S(2)}) collective-permute-start(f32[264,1024]{1,0:T(8,128)S(1)} %get-tuple-element.21), channel_id=1, source_target_pairs={{0,1},{1,0},{2,3},{3,2},{4,5},{5,4},{6,7},{7,6},{8,9},{9,8},{10,11... | collective-permute-start | bytes 3244040 | tf_op jit(solution)/shard_map/ppermute | solution.py:356
  11.7 0.0 copy-done.4
  11.7 3.3 %shard_map.145 = (f32[256,1024]{1,0:T(8,128)S(1)}, f32[256,256]{1,0:T(8,128)S(1)}, f32[32,256]{1,0:T(8,128)S(1)}, f32[40,256]{1,0:T(8,128)S(1)}) custom-call(s32[1,256]{1,0:T(1,128)S(1)} %copy-done.4, f32[104,256]{1,0:T(8,128)S(1)} %get-tuple-element.22.heads_ref, bf16[1,256,1024]{2,1,0:T(8,128)(2,1)S(1)} %get-tuple-element.23.x_ref, ...), custom_call_target="tpu_custom_call" | custom-call | flops 2000000000 | bytes 4194304 | tf_op jit(solution)/shard_map/pallas_call | solution.py:357
  14.9 0.0 copy-start
  15.0 0.0 copy-start.2
  15.0 0.0 collective-permute-done.got_ref
  15.0 0.0 copy-start.5
  15.0 1.3 %shard_map.147 = f32[1,128]{1,0:T(1,128)S(1)} custom-call(f32[264,1024]{1,0:T(8,128)S(1)} %collective-permute-done.got_ref, f32[104,256]{1,0:T(8,128)S(1)} %get-tuple-element.22.heads_ref, f32[40,256]{1,0:T(8,128)S(1)} %get-tuple-element.34.aux_ref, bf16[1,256,1024]{2,1,0:T(8,128)(2,1)S(1)} %get-tuple-element.23.x_ref, ...), custom_call_target="tpu_custom_call" | custom-call | flops 300000000 | bytes 2097152 | tf_op jit(solution)/shard_map/pallas_call | solution.py:364
  16.2 0.0 copy-done
  16.2 0.0 copy-done.2
  16.2 1.8 %all-gather = f32[2,1,128]{2,1,0:T(1,128)S(1)} all-gather(f32[1,1,128]{2,1,0:T(1,128)S(1)} %bitcast.10), channel_id=1, replica_groups=mesh['dp'=256,'ctx'=2] {'ctx'}, dimensions={0}, use_global_device_ids=true | all-gather | bytes 1536 | tf_op jit(solution)/shard_map/all_gather | solution.py:330
  18.0 0.7 %broadcast_in_dim.17 = f32[256,1,128]{2,1,0:T(1,128)} broadcast(f32[128]{0:T(128)S(1)} %fusion), dimensions={2} | broadcast | bytes 131584 | tf_op jit(solution)/shard_map/broadcast_in_dim | solution.py:332
  18.7 18.1 %all-to-all-start = ((f32[256,1,128]{2,1,0:T(1,128)}), f32[256,1,128]{2,1,0:T(1,128)}, u32[]{:S(2)}, u32[]{:S(2)}) async-start(f32[256,1,128]{2,1,0:T(1,128)} %broadcast_in_dim.17), calls=%async_computation | async-start | bytes 262144 | tf_op jit(solution)/shard_map/all_to_all | solution.py:333
  36.8 0.0 copy-done.5
  36.8 0.0 copy-start.1
  36.8 0.9 %copy-done.1 = f32[256,256]{1,0:T(8,128)S(1)} copy-done((f32[256,256]{1,0:T(8,128)S(1)}, f32[256,256]{1,0:T(8,128)}, u32[]{:S(2)}) %copy-start.1) | copy-done | bytes 262168
  37.8 0.0 copy-start.3
  37.8 0.8 %copy-done.3 = f32[32,256]{1,0:T(8,128)S(1)} copy-done((f32[32,256]{1,0:T(8,128)S(1)}, f32[32,256]{1,0:T(8,128)}, u32[]{:S(2)}) %copy-start.3) | copy-done | bytes 32792
  38.5 2.5 %shard_map.146 = (bf16[1,256,1024]{2,1,0:T(8,128)(2,1)}, bf16[1,256,256]{2,1,0:T(8,128)(2,1)}, bf16[1,256,256]{2,1,0:T(8,128)(2,1)}, f32[1,16,256]{2,1,0:T(8,128)}) custom-call(f32[264,1024]{1,0:T(8,128)S(1)} %collective-permute-done.got_ref, f32[104,256]{1,0:T(8,128)S(1)} %get-tuple-element.22.heads_ref, f32[32,256]{1,0:T(8,128)S(1)} %copy-done.3, ...), custom_call_target="tpu_custom_call" | custom-call | flops 1000000000 | bytes 5242880 | tf_op jit(solution)/shard_map/pallas_call | solution.py:371
  41.1 7.3 %all-to-all-done = f32[256,1,128]{2,1,0:T(1,128)} async-done(((f32[256,1,128]{2,1,0:T(1,128)}), f32[256,1,128]{2,1,0:T(1,128)}, u32[]{:S(2)}, u32[]{:S(2)}) %all-to-all-start) | async-done | bytes 131104 | tf_op jit(solution)/shard_map/all_to_all | solution.py:333
  48.4 1.0 %reduce_sum.9 = f32[128]{0:T(128)S(1)} reduce(f32[256,1,128]{2,0,1:T(8,128)} %bitcast.7, f32[]{:T(128)} %constant.0.clone.1), dimensions={0,1}, to_apply=%region_0.0 | reduce | flops 32640 | bytes 131588 | tf_op jit(solution)/shard_map/reduce_sum | solution.py:334
  49.3 0.6 %fusion.1 = (f32[16]{0:T(128)}, f32[16]{0:T(128)}, f32[16]{0:T(128)}) fusion(f32[128]{0:T(128)S(1)} %reduce_sum.9), kind=kLoop, calls=%fused_computation.2 | loop fusion | bytes 384 | tf_op jit(solution)/shard_map/slice | solution.py:384
  (1 shorter events, 0.0 us)
Async XLA Ops:
  0.6 11.0 %copy-start.4 = (s32[1,256]{1,0:T(1,128)S(1)}, s32[1,256]{1,0:T(1,128)}, u32[]{:S(2)}) copy-start(s32[1,256]{1,0:T(1,128)} %doc_ref.1) | copy-start | bytes 3076
  2.9 12.1 %collective-permute-start = (f32[264,1024]{1,0:T(8,128)S(1)}, f32[264,1024]{1,0:T(8,128)S(1)}, u32[]{:S(2)}, u32[]{:S(2)}) collective-permute-start(f32[264,1024]{1,0:T(8,128)S(1)} %get-tuple-element.21), channel_id=1, source_target_pairs={{0,1},{1,0},{2,3},{3,2},{4,5},{5,4},{6,7},{7,6},{8,9},{9,8},{10,11... | collective-permute-start | bytes 3244040 | tf_op jit(solution)/shard_map/ppermute | solution.py:356
  14.9 1.3 %copy-start = (f32[256,256]{1,0:T(8,128)}, f32[256,256]{1,0:T(8,128)S(1)}, u32[]{:S(2)}) copy-start(f32[256,256]{1,0:T(8,128)S(1)} %get-tuple-element.29.dp_ref) | copy-start | bytes 786436
  15.0 1.3 %copy-start.2 = (f32[32,256]{1,0:T(8,128)}, f32[32,256]{1,0:T(8,128)S(1)}, u32[]{:S(2)}) copy-start(f32[32,256]{1,0:T(8,128)S(1)} %get-tuple-element.27.stat_ref) | copy-start | bytes 98308
  15.0 21.9 %copy-start.5 = (f32[16]{0:T(128)S(1)}, f32[16]{0:T(128)}, u32[]{:S(2)}) copy-start(f32[16]{0:T(128)} %param.17) | copy-start | bytes 196
  18.7 29.6 %all-to-all-start = ((f32[256,1,128]{2,1,0:T(1,128)}), f32[256,1,128]{2,1,0:T(1,128)}, u32[]{:S(2)}, u32[]{:S(2)}) async-start(f32[256,1,128]{2,1,0:T(1,128)} %broadcast_in_dim.17), calls=%async_computation | async-start | bytes 262144 | tf_op jit(solution)/shard_map/all_to_all | solution.py:333
  36.8 1.0 %copy-start.1 = (f32[256,256]{1,0:T(8,128)S(1)}, f32[256,256]{1,0:T(8,128)}, u32[]{:S(2)}) copy-start(f32[256,256]{1,0:T(8,128)} %copy-done) | copy-start | bytes 786436
  37.8 0.8 %copy-start.3 = (f32[32,256]{1,0:T(8,128)S(1)}, f32[32,256]{1,0:T(8,128)}, u32[]{:S(2)}) copy-start(f32[32,256]{1,0:T(8,128)} %copy-done.2) | copy-start | bytes 98308

commit v4 on v3

--- a/solution.py
+++ b/solution.py
@@ -109,8 +109,8 @@
 PART = WIDTH // PARTS
 STEP, GAIN, SIG, ELL, CUM, CUM_SIG, EDGE = (HEADS * n for n in range(7))
 KEPT = EDGE + 8
-COL, ROW = 0, HEADS
 W_RATE, W_BIAS, OWN = 0, HEADS, 2 * HEADS
+COL, ROW, PAIRS = OWN + 8, OWN + 8 + HEADS, OWN + 8 + 2 * HEADS
 
 
 def outgoing_kernel(
@@ -194,7 +194,7 @@
 
 def intra_kernel(
     doc_ref, heads_ref, x_ref, c_ref, w_ref, r_ref,
-    dx_ref, dp_ref, stat_ref, aux_ref,
+    dx_ref, aux_ref,
     mask_ref, p_ref,
 ):
     first = lax.axis_index("ctx") == 0
@@ -209,6 +209,7 @@
         ok = (i >= j) & (doc_col == doc[:, span])
         mask_ref[:, span] = jnp.where(ok, 0.0, NEG)
     p_ref[...] = dot(w_ref[0], r_ref[0], NT)
+    dp_ref = aux_ref.at[PAIRS:]
     dp_ref[...] = jnp.zeros((BLOCK, BLOCK), F32)
     rows2 = cum * LOG2E
     cols2 = jnp.concatenate([(cum - jnp.log(s)) * LOG2E, jnp.zeros((128 - HEADS, BLOCK), F32)], axis=0).T
@@ -233,8 +234,8 @@
 
             d0, e0 = tile(slice(0, HALF), slice(0, BLOCK))
             d1, e1 = tile(slice(HALF, BLOCK), slice(HALF, BLOCK))
-            stat_ref[ROW + h : ROW + h + 1, 0:HALF] = e0[:, 0:HALF]
-            stat_ref[ROW + h : ROW + h + 1, HALF:] = e0[:, HALF:] + e1
+            aux_ref[ROW + h : ROW + h + 1, 0:HALF] = e0[:, 0:HALF]
+            aux_ref[ROW + h : ROW + h + 1, HALF:] = e0[:, HALF:] + e1
             top = d0 if top is None else top + d0
             bottom = d1 if bottom is None else bottom + d1
         dx_ref[0:HALF, lanes] = top
@@ -242,10 +243,10 @@
     rows = head_rows(HEADS)
     x = x_ref[0].astype(F32)
     q = head_sums(x * dx_ref[...], rows)
-    stat_ref[COL:ROW] = q
+    aux_ref[COL:ROW] = q
     cx = jnp.sum(c_ref[0].astype(F32) * x, axis=0, keepdims=True)
     skip = sum(dot(rows, part, NT) for part in split3(jnp.broadcast_to(cx, (128, WIDTH))))
-    da = stat_ref[ROW:] - q
+    da = aux_ref[ROW:PAIRS] - q
     over = sig / s
     own_rate = jnp.sum(da * cum, axis=1, keepdims=True)
     own_bias = jnp.sum(q * over - ell * (da * cum_sig), axis=1, keepdims=True)
@@ -255,7 +256,7 @@
     w_bias = jnp.where(first, over + ell * (cum_sig - cum_sig[:, BLOCK - 1 :]), -ell * cum_sig)
     aux_ref[W_RATE:W_BIAS] = f * w_rate
     aux_ref[W_BIAS:OWN] = f * w_bias
-    aux_ref[OWN:] = jnp.broadcast_to(own, (8, BLOCK))
+    aux_ref[OWN:COL] = jnp.broadcast_to(own, (8, BLOCK))
 
 
 def joined(got_ref, heads_ref):
@@ -277,32 +278,41 @@
 
 
 def grads_kernel(
-    got_ref, heads_ref, stat_ref, skip_ref, x_ref, c_ref, w_ref, r_ref, dxi_ref, dp_ref,
+    got_ref, heads_ref, aux_ref, skip_ref, dxi_ref, x_hbm, c_hbm, w_hbm, r_hbm,
     dx_ref, dw_ref, dr_ref, dstep_ref,
+    x_ref, c_ref, w_ref, r_ref, sems,
 ):
+    pairs = ((w_hbm, w_ref), (r_hbm, r_ref), (x_hbm, x_ref), (c_hbm, c_ref))
+    copies = [pltpu.make_async_copy(src, dst, sems.at[n]) for n, (src, dst) in enumerate(pairs)]
+    for copy in copies:
+        copy.start()
     first = lax.axis_index("ctx") == 0
     f = heads_ref[GAIN:SIG] * joined(got_ref, heads_ref)
     wide = dot(pieces(f), head_rows(128))
+    gains = dot(pieces(jnp.broadcast_to(to_column(skip_ref[...]), (HEADS, BLOCK))), head_rows(128))
+    t_hi, t_lo = split2(got_ref[0:STATE])
+    for copy in copies[0:2]:
+        copy.wait()
+    k = jnp.where(first, w_ref[0], r_ref[0])
+    zs = (dot(k, t_hi) + dot(k, t_lo)) * wide
+    hi, lo = split2(aux_ref[PAIRS:])
+    dw = dot(hi, r_ref[0]) + dot(lo, r_ref[0])
+    hi, lo = split2(aux_ref[PAIRS:].T)
+    dr = dot(hi, w_ref[0]) + dot(lo, w_ref[0])
+    for copy in copies[2:]:
+        copy.wait()
     c = c_ref[0].astype(F32)
     v = jnp.where(first, x_ref[0], c_ref[0]).astype(F32)
-    k = jnp.where(first, w_ref[0], r_ref[0])
-    t_hi, t_lo = split2(got_ref[0:STATE])
-    zs = (dot(k, t_hi) + dot(k, t_lo)) * wide
     hi, lo = split2(v * wide)
     dk = dot(hi, t_hi, NT) + dot(lo, t_hi, NT) + dot(hi, t_lo, NT)
     zero = jnp.zeros_like(dk)
-    hi, lo = split2(dp_ref[...])
-    dw = dot(hi, r_ref[0]) + dot(lo, r_ref[0])
-    hi, lo = split2(dp_ref[...].T)
-    dr = dot(hi, w_ref[0]) + dot(lo, w_ref[0])
     dw_ref[0] = (dw + jnp.where(first, dk, zero)).astype(BF16)
     dr_ref[0] = (dr + jnp.where(first, zero, dk)).astype(BF16)
-    gains = dot(pieces(jnp.broadcast_to(to_column(skip_ref[...]), (HEADS, BLOCK))), head_rows(128))
     dx = dxi_ref[...] + jnp.where(first, zs, 0.0) + gains * c
     dx_ref[0] = dx.astype(BF16)
     u = head_sums(v * zs, head_rows(HEADS))
-    q = stat_ref[COL:ROW] + jnp.where(first, u, 0.0)
-    da = stat_ref[ROW:] - q + jnp.where(first, 0.0, u)
+    q = aux_ref[COL:ROW] + jnp.where(first, u, 0.0)
+    da = aux_ref[ROW:PAIRS] - q + jnp.where(first, 0.0, u)
     drate = along_tokens(da, triangle(False))
     drate = drate + jnp.where(first, jnp.sum(u, axis=1, keepdims=True), 0.0)
     dstep = (q / heads_ref[STEP:GAIN] - drate * heads_ref[ELL:CUM]) * heads_ref[SIG:ELL]
@@ -354,9 +364,9 @@
         in_specs=[pl.BlockSpec(memory_space=pltpu.HBM)] * 8,
     )(*inputs)
     got = lax.ppermute(send, "ctx", [(0, 1), (1, 0)])
-    dxi, dp, stat, aux = call(
+    dxi, aux = call(
         intra_kernel,
-        (shape((BLOCK, WIDTH)), shape((BLOCK, BLOCK)), shape((2 * HEADS, BLOCK)), shape((OWN + 8, BLOCK))),
+        (shape((BLOCK, WIDTH)), shape((PAIRS + BLOCK, BLOCK))),
         scratch=[pltpu.VMEM((BLOCK, BLOCK), F32)] * 2,
         flops=2_000_000_000,
         bytes_accessed=4 << 20,
@@ -376,9 +386,13 @@
             shape((1, BLOCK, STATE), BF16),
             shape((1, HEADS, BLOCK)),
         ),
+        scratch=[pltpu.VMEM((1, BLOCK, WIDTH), BF16)] * 2
+        + [pltpu.VMEM((1, BLOCK, STATE), BF16)] * 2
+        + [pltpu.SemaphoreType.DMA((4,))],
         flops=1_000_000_000,
         bytes_accessed=5 << 20,
-    )(got, heads, stat, skip, x, c, w, r, dxi, dp)
+        in_specs=[pl.BlockSpec(memory_space=pltpu.VMEM)] * 5 + [pl.BlockSpec(memory_space=pltpu.HBM)] * 4,
+    )(got, heads, aux, skip, dxi, *inputs[4:])
     return (
         grad_x, grad_w, grad_r, grad_step.swapaxes(1, 2),
         total[0:HEADS], total[HEADS : 2 * HEADS], total[2 * HEADS : 3 * HEADS],

time: 50.3 us -> 48.7 us (0.968)
  local copies, waits for them, and re-layouts: 3.06 us -> 1.32 us
  Pallas kernels: 9.27 us -> 10.4 us
  waiting for transfers between devices: 7.3 us -> 8.42 us
  starting transfers between devices: 26.9 us -> 25.8 us
  other arithmetic: 0.95 us -> 0.05 us
    unnamed x12 -> x4, local copies, waits for them, and re-layouts: 1.72 us -> 0.01 us
    all_to_all x1, waiting for transfers between devices: 7.3 us -> 8.42 us  [mesh_sum(): lax.all_to_all(everyone, 'dp', split_axis=0, concat_axis=0, tiled=True)]
    pallas_call x1, Pallas kernels: 2.52 us -> 3.63 us  [on_device(): call(grads_kernel, (shape((1, BLOCK, WIDTH), BF16), shape((1, BLOCK, STAT...]
    all_to_all x1, starting transfers between devices: 18.1 us -> 17 us  [mesh_sum(): lax.all_to_all(everyone, 'dp', split_axis=0, concat_axis=0, tiled=True)]
    reduce_sum x1, other arithmetic: 0.95 us -> 0.05 us  [mesh_sum(): return jnp.sum(everyone, axis=0)]
  transfers between devices with their start and end apart: 2 -> 2, of which waited for: 1 -> 1; matrix products, arithmetic and copies ran while one was open for 0% -> 0% of each run, Pallas kernels for 12% -> 14%
where the time goes in v4:
time: 48.7 us; the launch traced here: 48.4 us
  starting transfers between devices  25.8 us (53%)
  Pallas kernels  10.4 us (21%)
  waiting for transfers between devices  8.42 us (17%)
  blocking collectives  1.76 us (4%)
  local copies, waits for them, and re-layouts  1.32 us (3%)
  between operations  0.69 us (1%)
    all_to_all x1, starting transfers between devices, mesh_sum(): lax.all_to_all(everyone, 'dp', split_axis=0, concat_axis=0, tiled=True)  17 us
    ppermute x1, starting transfers between devices, on_device(): got = lax.ppermute(send, 'ctx', [(0, 1), (1, 0)])  8.79 us
    all_to_all x1, waiting for transfers between devices, mesh_sum(): lax.all_to_all(everyone, 'dp', split_axis=0, concat_axis=0, tiled=True)  8.42 us
    pallas_call x1, Pallas kernels, on_device(): call(grads_kernel, (shape((1, BLOCK, WIDTH), BF16), shape((1, BLOCK, STAT...  3.63 us
    pallas_call x1, Pallas kernels, on_device(): call(intra_kernel, (shape((BLOCK, WIDTH)), shape((PAIRS + BLOCK, BLOCK)))...  3.27 us
    pallas_call x1, Pallas kernels, on_device(): call(outgoing_kernel, (shape((STATE + 8, WIDTH)), shape((KEPT, BLOCK)), r...  2.22 us
    all_gather x1, blocking collectives, mesh_sum(): both = lax.all_gather(sums, 'ctx', axis=0, tiled=True)  1.76 us
    pallas_call x1, Pallas kernels, on_device(): call(sums_kernel, shape((1, 128)), flops=300000000, bytes_accessed=2 << 20)  1.27 us
  transfers between devices with their start and end apart: 2, of which 1 were waited for; matrix products, arithmetic and copies ran while one was open for 0% of the time, Pallas kernels for 14%

profile of v4, /device:TPU:1, one launch (start us, length us, event | category | flops | bytes accessed | tf_op | source)
XLA Modules:
  0.0 48.4 jit_solution(17740399187344135450)
XLA Ops:
  0.6 0.0 copy-start
  0.6 2.2 %shard_map.144 = (f32[264,1024]{1,0:T(8,128)S(1)}, f32[104,256]{1,0:T(8,128)S(1)}, bf16[1,256,1024]{2,1,0:T(8,128)(2,1)S(1)}, bf16[1,256,1024]{2,1,0:T(8,128)(2,...) custom-call(s32[1,256]{1,0:T(1,128)} %doc_ref.1, f32[1,16,256]{2,1,0:T(8,128)} %bitcast.12, ...), custom_call_target="tpu_custom_call" | custom-call | flops 300000000 | bytes 2097152 | tf_op jit(solution)/shard_map/pallas_call | solution.py:352
  2.9 8.8 %collective-permute-start = (f32[264,1024]{1,0:T(8,128)S(1)}, f32[264,1024]{1,0:T(8,128)S(1)}, u32[]{:S(2)}, u32[]{:S(2)}) collective-permute-start(f32[264,1024]{1,0:T(8,128)S(1)} %get-tuple-element.19), channel_id=1, source_target_pairs={{0,1},{1,0},{2,3},{3,2},{4,5},{5,4},{6,7},{7,6},{8,9},{9,8},{10,11... | collective-permute-start | bytes 3244040 | tf_op jit(solution)/shard_map/ppermute | solution.py:366
  11.7 0.0 copy-done
  11.7 3.3 %shard_map.145 = (f32[256,1024]{1,0:T(8,128)S(1)}, f32[328,256]{1,0:T(8,128)S(1)}) custom-call(s32[1,256]{1,0:T(1,128)S(1)} %copy-done, f32[104,256]{1,0:T(8,128)S(1)} %get-tuple-element.20.heads_ref, bf16[1,256,1024]{2,1,0:T(8,128)(2,1)S(1)} %get-tuple-element.21.x_ref, bf16[1,256,1024]{2,1,0:T(8,128)(2,1)S(1)} %get-tuple-element.22.c_ref, ...), custom_call_target="tpu_custom_call" | custom-call | flops 2000000000 | bytes 4194304 | tf_op jit(solution)/shard_map/pallas_call | solution.py:367
  15.0 0.0 collective-permute-done.got_ref
  15.0 0.0 copy-start.1
  15.0 1.3 %shard_map.147 = f32[1,128]{1,0:T(1,128)S(1)} custom-call(f32[264,1024]{1,0:T(8,128)S(1)} %collective-permute-done.got_ref, f32[104,256]{1,0:T(8,128)S(1)} %get-tuple-element.20.heads_ref, f32[328,256]{1,0:T(8,128)S(1)} %get-tuple-element.25.aux_ref, bf16[1,256,1024]{2,1,0:T(8,128)(2,1)S(1)} %get-tuple-element.21.x_ref, ...), custom_call_target="tpu_custom_call" | custom-call | flops 300000000 | bytes 2097152 | tf_op jit(solution)/shard_map/pallas_call | solution.py:374
  16.2 1.8 %all-gather = f32[2,1,128]{2,1,0:T(1,128)S(1)} all-gather(f32[1,1,128]{2,1,0:T(1,128)S(1)} %bitcast.10), channel_id=1, replica_groups=mesh['dp'=256,'ctx'=2] {'ctx'}, dimensions={0}, use_global_device_ids=true | all-gather | bytes 1536 | tf_op jit(solution)/shard_map/all_gather | solution.py:340
  18.0 0.7 %broadcast_in_dim.17 = f32[256,1,128]{2,1,0:T(1,128)} broadcast(f32[128]{0:T(128)S(1)} %fusion), dimensions={2} | broadcast | bytes 131584 | tf_op jit(solution)/shard_map/broadcast_in_dim | solution.py:342
  18.7 17.0 %all-to-all-start = ((f32[256,1,128]{2,1,0:T(1,128)}), f32[256,1,128]{2,1,0:T(1,128)S(1)}, u32[]{:S(2)}, u32[]{:S(2)}) async-start(f32[256,1,128]{2,1,0:T(1,128)} %broadcast_in_dim.17), calls=%async_computation | async-start | bytes 262144 | tf_op jit(solution)/shard_map/all_to_all | solution.py:343
  35.7 0.0 copy-done.1
  35.7 3.6 %shard_map.146 = (bf16[1,256,1024]{2,1,0:T(8,128)(2,1)}, bf16[1,256,256]{2,1,0:T(8,128)(2,1)}, bf16[1,256,256]{2,1,0:T(8,128)(2,1)}, f32[1,16,256]{2,1,0:T(8,128)}) custom-call(f32[264,1024]{1,0:T(8,128)S(1)} %collective-permute-done.got_ref, f32[104,256]{1,0:T(8,128)S(1)} %get-tuple-element.20.heads_ref, f32[328,256]{1,0:T(8,128)S(1)} %get-tuple-element.25.aux_ref, ...), custom_call_target="tpu_custom_call" | custom-call | flops 1000000000 | bytes 5242880 | tf_op jit(solution)/shard_map/pallas_call | solution.py:381
  39.4 8.4 %all-to-all-done = f32[256,1,128]{2,1,0:T(1,128)S(1)} async-done(((f32[256,1,128]{2,1,0:T(1,128)}), f32[256,1,128]{2,1,0:T(1,128)S(1)}, u32[]{:S(2)}, u32[]{:S(2)}) %all-to-all-start) | async-done | bytes 131104 | tf_op jit(solution)/shard_map/all_to_all | solution.py:343
  47.8 0.6 %fusion.1 = (f32[16]{0:T(128)}, f32[16]{0:T(128)}, f32[16]{0:T(128)}) fusion(f32[128]{0:T(128)S(1)} %reduce_sum.9), kind=kLoop, calls=%fused_computation.2 | loop fusion | bytes 384 | tf_op jit(solution)/shard_map/slice | solution.py:398
  (2 shorter events, 0.1 us)
Async XLA Ops:
  0.6 11.0 %copy-start = (s32[1,256]{1,0:T(1,128)S(1)}, s32[1,256]{1,0:T(1,128)}, u32[]{:S(2)}) copy-start(s32[1,256]{1,0:T(1,128)} %doc_ref.1) | copy-start | bytes 3076
  2.9 12.1 %collective-permute-start = (f32[264,1024]{1,0:T(8,128)S(1)}, f32[264,1024]{1,0:T(8,128)S(1)}, u32[]{:S(2)}, u32[]{:S(2)}) collective-permute-start(f32[264,1024]{1,0:T(8,128)S(1)} %get-tuple-element.19), channel_id=1, source_target_pairs={{0,1},{1,0},{2,3},{3,2},{4,5},{5,4},{6,7},{7,6},{8,9},{9,8},{10,11... | collective-permute-start | bytes 3244040 | tf_op jit(solution)/shard_map/ppermute | solution.py:366
  15.0 20.8 %copy-start.1 = (f32[16]{0:T(128)S(1)}, f32[16]{0:T(128)}, u32[]{:S(2)}) copy-start(f32[16]{0:T(128)} %param.17) | copy-start | bytes 196
  18.7 29.1 %all-to-all-start = ((f32[256,1,128]{2,1,0:T(1,128)}), f32[256,1,128]{2,1,0:T(1,128)S(1)}, u32[]{:S(2)}, u32[]{:S(2)}) async-start(f32[256,1,128]{2,1,0:T(1,128)} %broadcast_in_dim.17), calls=%async_computation | async-start | bytes 262144 | tf_op jit(solution)/shard_map/all_to_all | solution.py:343

commit v5 on v4

--- a/solution.py
+++ b/solution.py
@@ -106,6 +106,7 @@
 
 
 PARTS = 4
+FETCHES = 1
 PART = WIDTH // PARTS
 STEP, GAIN, SIG, ELL, CUM, CUM_SIG, EDGE = (HEADS * n for n in range(7))
 KEPT = EDGE + 8
@@ -134,12 +135,12 @@
         copy.start()
 
     def rows_of(src, dst, base):
-        part = BLOCK // PARTS
-        spans = [pl.ds(n * part, part) for n in range(PARTS)]
+        part = BLOCK // FETCHES
+        spans = [pl.ds(n * part, part) for n in range(FETCHES)]
         return [fetch(src.at[:, span], dst.at[:, span], base + n) for n, span in enumerate(spans)]
 
     fetch_w, fetch_r = fetch(w_hbm, w_ref, 4), fetch(r_hbm, r_ref, 5)
-    fetch_x, fetch_c = rows_of(x_hbm, x_ref, 6), rows_of(c_hbm, c_ref, 6 + PARTS)
+    fetch_x, fetch_c = rows_of(x_hbm, x_ref, 6), rows_of(c_hbm, c_ref, 6 + FETCHES)
 
     @pl.when(first)
     def _():
@@ -217,29 +218,31 @@
     for pair in range(HEADS // 2):
         lanes = slice(pair * PAIR, (pair + 1) * PAIR)
         xp, cp = x_ref[0, :, lanes], c_ref[0, :, lanes]
-        top = bottom = None
+        top = None
         for odd in range(2):
             h = 2 * pair + odd
             ch = jnp.where((lane < HEAD_DIM) != bool(odd), cp, jnp.zeros_like(cp))
             row = rows2[h : h + 1, :]
             col = cols2[:, h : h + 1]
 
+            g = dot(xp, ch, NT)
+
             def tile(js, isl):
-                g = dot(xp[js], ch[isl], NT)
                 decay = jnp.exp2((row[:, isl] - col[js]) + mask_ref[js, isl])
                 m = decay * p_ref[js, isl]
-                dp_ref[js, isl] += decay * g
-                hi, lo = split2(m)
-                return dot(hi, ch[isl]) + dot(lo, ch[isl]), jnp.sum(m * g, axis=0, keepdims=True)
-
-            d0, e0 = tile(slice(0, HALF), slice(0, BLOCK))
-            d1, e1 = tile(slice(HALF, BLOCK), slice(HALF, BLOCK))
+                dp_ref[js, isl] += decay * g[js, isl]
+                return split2(m), jnp.sum(m * g[js, isl], axis=0, keepdims=True)
+
+            (hi0, lo0), e0 = tile(slice(0, HALF), slice(0, BLOCK))
+            (hi1, lo1), e1 = tile(slice(HALF, BLOCK), slice(HALF, BLOCK))
+            zero = jnp.zeros_like(hi1)
+            hi1, lo1 = (jnp.concatenate([zero, part], axis=1) for part in (hi1, lo1))
+            d = dot(jnp.concatenate([hi0, hi1, lo0, lo1], axis=0), ch)
+            d = d[0:BLOCK] + d[BLOCK:]
             aux_ref[ROW + h : ROW + h + 1, 0:HALF] = e0[:, 0:HALF]
             aux_ref[ROW + h : ROW + h + 1, HALF:] = e0[:, HALF:] + e1
-            top = d0 if top is None else top + d0
-            bottom = d1 if bottom is None else bottom + d1
-        dx_ref[0:HALF, lanes] = top
-        dx_ref[HALF:, lanes] = bottom
+            top = d if top is None else top + d
+        dx_ref[:, lanes] = top
     rows = head_rows(HEADS)
     x = x_ref[0].astype(F32)
     q = head_sums(x * dx_ref[...], rows)
@@ -357,7 +360,7 @@
             pltpu.VMEM((1, HEADS, BLOCK), F32),
             pltpu.VMEM((1, HEADS), F32),
             pltpu.VMEM((1, HEADS), F32),
-            pltpu.SemaphoreType.DMA((6 + 2 * PARTS,)),
+            pltpu.SemaphoreType.DMA((6 + 2 * FETCHES,)),
         ),
         flops=300_000_000,
         bytes_accessed=2 << 20,

time: 48.7 us -> 48.3 us (level)
  no operation moved by 1% of the time
where the time goes in v5:
time: 48.3 us; the launch traced here: 48.1 us
  starting transfers between devices  25.8 us (53%)
  Pallas kernels  10.1 us (21%)
  waiting for transfers between devices  8.42 us (17%)
  blocking collectives  1.76 us (4%)
  local copies, waits for them, and re-layouts  1.32 us (3%)
  between operations  0.69 us (1%)
    all_to_all x1, starting transfers between devices, mesh_sum(): lax.all_to_all(everyone, 'dp', split_axis=0, concat_axis=0, tiled=True)  17 us
    ppermute x1, starting transfers between devices, on_device(): got = lax.ppermute(send, 'ctx', [(0, 1), (1, 0)])  8.79 us
    all_to_all x1, waiting for transfers between devices, mesh_sum(): lax.all_to_all(everyone, 'dp', split_axis=0, concat_axis=0, tiled=True)  8.42 us
    pallas_call x1, Pallas kernels, on_device(): call(grads_kernel, (shape((1, BLOCK, WIDTH), BF16), shape((1, BLOCK, STAT...  3.63 us
    pallas_call x1, Pallas kernels, on_device(): call(intra_kernel, (shape((BLOCK, WIDTH)), shape((PAIRS + BLOCK, BLOCK)))...  3 us
    pallas_call x1, Pallas kernels, on_device(): call(outgoing_kernel, (shape((STATE + 8, WIDTH)), shape((KEPT, BLOCK)), r...  2.15 us
    all_gather x1, blocking collectives, mesh_sum(): both = lax.all_gather(sums, 'ctx', axis=0, tiled=True)  1.76 us
    pallas_call x1, Pallas kernels, on_device(): call(sums_kernel, shape((1, 128)), flops=300000000, bytes_accessed=2 << 20)  1.27 us
  transfers between devices with their start and end apart: 2, of which 1 were waited for; matrix products, arithmetic and copies ran while one was open for 0% of the time, Pallas kernels for 14%

profile of v5, /device:TPU:1, one launch (start us, length us, event | category | flops | bytes accessed | tf_op | source)
XLA Modules:
  0.0 48.1 jit_solution(3053776493980258748)
XLA Ops:
  0.6 0.0 copy-start
  0.6 2.2 %shard_map.144 = (f32[264,1024]{1,0:T(8,128)S(1)}, f32[104,256]{1,0:T(8,128)S(1)}, bf16[1,256,1024]{2,1,0:T(8,128)(2,1)S(1)}, bf16[1,256,1024]{2,1,0:T(8,128)(2,...) custom-call(s32[1,256]{1,0:T(1,128)} %doc_ref.1, f32[1,16,256]{2,1,0:T(8,128)} %bitcast.12, ...), custom_call_target="tpu_custom_call" | custom-call | flops 300000000 | bytes 2097152 | tf_op jit(solution)/shard_map/pallas_call | solution.py:355
  2.8 8.8 %collective-permute-start = (f32[264,1024]{1,0:T(8,128)S(1)}, f32[264,1024]{1,0:T(8,128)S(1)}, u32[]{:S(2)}, u32[]{:S(2)}) collective-permute-start(f32[264,1024]{1,0:T(8,128)S(1)} %get-tuple-element.19), channel_id=1, source_target_pairs={{0,1},{1,0},{2,3},{3,2},{4,5},{5,4},{6,7},{7,6},{8,9},{9,8},{10,11... | collective-permute-start | bytes 3244040 | tf_op jit(solution)/shard_map/ppermute | solution.py:369
  11.6 0.0 copy-done
  11.6 3.0 %shard_map.145 = (f32[256,1024]{1,0:T(8,128)S(1)}, f32[328,256]{1,0:T(8,128)S(1)}) custom-call(s32[1,256]{1,0:T(1,128)S(1)} %copy-done, f32[104,256]{1,0:T(8,128)S(1)} %get-tuple-element.20.heads_ref, bf16[1,256,1024]{2,1,0:T(8,128)(2,1)S(1)} %get-tuple-element.21.x_ref, bf16[1,256,1024]{2,1,0:T(8,128)(2,1)S(1)} %get-tuple-element.22.c_ref, ...), custom_call_target="tpu_custom_call" | custom-call | flops 2000000000 | bytes 4194304 | tf_op jit(solution)/shard_map/pallas_call | solution.py:370
  14.6 0.0 collective-permute-done.got_ref
  14.6 0.0 copy-start.1
  14.6 1.3 %shard_map.147 = f32[1,128]{1,0:T(1,128)S(1)} custom-call(f32[264,1024]{1,0:T(8,128)S(1)} %collective-permute-done.got_ref, f32[104,256]{1,0:T(8,128)S(1)} %get-tuple-element.20.heads_ref, f32[328,256]{1,0:T(8,128)S(1)} %get-tuple-element.25.aux_ref, bf16[1,256,1024]{2,1,0:T(8,128)(2,1)S(1)} %get-tuple-element.21.x_ref, ...), custom_call_target="tpu_custom_call" | custom-call | flops 300000000 | bytes 2097152 | tf_op jit(solution)/shard_map/pallas_call | solution.py:377
  15.9 1.8 %all-gather = f32[2,1,128]{2,1,0:T(1,128)S(1)} all-gather(f32[1,1,128]{2,1,0:T(1,128)S(1)} %bitcast.10), channel_id=1, replica_groups=mesh['dp'=256,'ctx'=2] {'ctx'}, dimensions={0}, use_global_device_ids=true | all-gather | bytes 1536 | tf_op jit(solution)/shard_map/all_gather | solution.py:343
  17.7 0.7 %broadcast_in_dim.17 = f32[256,1,128]{2,1,0:T(1,128)} broadcast(f32[128]{0:T(128)S(1)} %fusion), dimensions={2} | broadcast | bytes 131584 | tf_op jit(solution)/shard_map/broadcast_in_dim | solution.py:345
  18.4 17.0 %all-to-all-start = ((f32[256,1,128]{2,1,0:T(1,128)}), f32[256,1,128]{2,1,0:T(1,128)S(1)}, u32[]{:S(2)}, u32[]{:S(2)}) async-start(f32[256,1,128]{2,1,0:T(1,128)} %broadcast_in_dim.17), calls=%async_computation | async-start | bytes 262144 | tf_op jit(solution)/shard_map/all_to_all | solution.py:346
  35.4 0.0 copy-done.1
  35.4 3.6 %shard_map.146 = (bf16[1,256,1024]{2,1,0:T(8,128)(2,1)}, bf16[1,256,256]{2,1,0:T(8,128)(2,1)}, bf16[1,256,256]{2,1,0:T(8,128)(2,1)}, f32[1,16,256]{2,1,0:T(8,128)}) custom-call(f32[264,1024]{1,0:T(8,128)S(1)} %collective-permute-done.got_ref, f32[104,256]{1,0:T(8,128)S(1)} %get-tuple-element.20.heads_ref, f32[328,256]{1,0:T(8,128)S(1)} %get-tuple-element.25.aux_ref, ...), custom_call_target="tpu_custom_call" | custom-call | flops 1000000000 | bytes 5242880 | tf_op jit(solution)/shard_map/pallas_call | solution.py:384
  39.0 8.4 %all-to-all-done = f32[256,1,128]{2,1,0:T(1,128)S(1)} async-done(((f32[256,1,128]{2,1,0:T(1,128)}), f32[256,1,128]{2,1,0:T(1,128)S(1)}, u32[]{:S(2)}, u32[]{:S(2)}) %all-to-all-start) | async-done | bytes 131104 | tf_op jit(solution)/shard_map/all_to_all | solution.py:346
  47.5 0.6 %fusion.1 = (f32[16]{0:T(128)}, f32[16]{0:T(128)}, f32[16]{0:T(128)}) fusion(f32[128]{0:T(128)S(1)} %reduce_sum.9), kind=kLoop, calls=%fused_computation.2 | loop fusion | bytes 384 | tf_op jit(solution)/shard_map/slice | solution.py:401
  (2 shorter events, 0.1 us)
Async XLA Ops:
  0.6 11.0 %copy-start = (s32[1,256]{1,0:T(1,128)S(1)}, s32[1,256]{1,0:T(1,128)}, u32[]{:S(2)}) copy-start(s32[1,256]{1,0:T(1,128)} %doc_ref.1) | copy-start | bytes 3076
  2.8 11.8 %collective-permute-start = (f32[264,1024]{1,0:T(8,128)S(1)}, f32[264,1024]{1,0:T(8,128)S(1)}, u32[]{:S(2)}, u32[]{:S(2)}) collective-permute-start(f32[264,1024]{1,0:T(8,128)S(1)} %get-tuple-element.19), channel_id=1, source_target_pairs={{0,1},{1,0},{2,3},{3,2},{4,5},{5,4},{6,7},{7,6},{8,9},{9,8},{10,11... | collective-permute-start | bytes 3244040 | tf_op jit(solution)/shard_map/ppermute | solution.py:369
  14.6 20.8 %copy-start.1 = (f32[16]{0:T(128)S(1)}, f32[16]{0:T(128)}, u32[]{:S(2)}) copy-start(f32[16]{0:T(128)} %param.17) | copy-start | bytes 196
  18.4 29.1 %all-to-all-start = ((f32[256,1,128]{2,1,0:T(1,128)}), f32[256,1,128]{2,1,0:T(1,128)S(1)}, u32[]{:S(2)}, u32[]{:S(2)}) async-start(f32[256,1,128]{2,1,0:T(1,128)} %broadcast_in_dim.17), calls=%async_computation | async-start | bytes 262144 | tf_op jit(solution)/shard_map/all_to_all | solution.py:346
